TPU v7x, 32 devices: a whole 2x2x4 slice. The times are simulated.
32 devices in a mesh: tensor: 4 (over z), shard: 2 (over y), replica: 4 (over x, core).
Axes of the slice: x: 2, y: 2, z: 4, core: 2. Of those that a mesh axis runs over, the one named last changes fastest.
Arguments:
- block_in: float32 [8, 640, 1024], P(('shard', 'replica'), 'tensor'), may hold values from -12 to 12
- segment_ids: int32 [8, 640], P(('shard', 'replica')), may hold values from 0 to 3, never falling along the last dimension, each value on 1 to 256 neighbouring positions
- grad_out: float32 [8, 640, 1024], P(('shard', 'replica'), 'tensor'), may hold values from -6 to 6
- qkv_weight: bfloat16 [1024, 3, 1024], P('shard', None, 'tensor'), may hold values from -2 to 2
- qv_bias: bfloat16 [2, 1024], P(None, ('tensor', 'shard')), may hold values from -3 to 3
- out_weight: bfloat16 [1024, 1024], P('tensor', 'shard'), may hold values from -0.75 to 0.75
- up_weight: bfloat16 [1024, 4096], P('shard', 'tensor'), may hold values from -0.1875 to 0.1875
- up_bias: bfloat16 [4096], P(('tensor', 'shard')), may hold values from -3 to 3
- down_weight: bfloat16 [4096, 1024], P('tensor', 'shard'), may hold values from -0.09375 to 0.09375
- norm_gains: bfloat16 [2, 1024], P(None, 'shard'), may hold values from 0.25 to 1.75
- shift_biases: bfloat16 [4, 1024], P(None, 'shard'), may hold values from -3 to 3
Outputs:
- block_out: float32 [8, 640, 1024], P(('shard', 'replica'), 'tensor')
- grad_in: float32 [8, 640, 1024], P(('shard', 'replica'), 'tensor')
- grad_qkv_weight: float32 [1024, 3, 1024], P('shard', None, 'tensor')
- grad_qv_bias: float32 [2, 1024], P(None, ('tensor', 'shard'))
- grad_out_weight: float32 [1024, 1024], P('tensor', 'shard')
- grad_up_weight: float32 [1024, 4096], P('shard', 'tensor')
- grad_up_bias: float32 [4096], P(('tensor', 'shard'))
- grad_down_weight: float32 [4096, 1024], P('tensor', 'shard')
- grad_norm_gains: float32 [2, 1024], P(None, 'shard')
- grad_shift_biases: float32 [4, 1024], P(None, 'shard')
Inputs may be any that keep to these rules, and one draw needn't show every extreme that they name: segment_ids never fall along a sequence; a document has 1 to 256 tokens, and one has exactly 256.
All inputs are finite; a program needn't handle non-finite values.
Results may differ from a plain program's by a relative error of at most 0.009.
The roundings to bfloat16 on the way count: a program that leaves them out, or rounds other values in their place, can miss the bound.
Values may be sent and summed in bfloat16 or wider, within the bound.
A program may use at most 128 MiB of HBM per device.

v0:
```python
import math

import jax
import jax.numpy as jnp
from jax import lax
from jax.sharding import PartitionSpec as P

HEAD_DIM = 64


norm_eps = 1e-12
masked_score = -1e30


def norm_forward(summed, gain, shift):
    center = summed - jnp.mean(summed, axis=-1, keepdims=True)
    inverse = lax.rsqrt(jnp.mean(center * center, axis=-1, keepdims=True) + norm_eps)
    normed = center * inverse
    return (normed * gain + shift, normed, inverse)


def norm_backward(grad, normed, inverse, gain):
    scaled = grad * gain
    return inverse * (
        scaled
        - jnp.mean(scaled, axis=-1, keepdims=True)
        - normed * jnp.mean(scaled * normed, axis=-1, keepdims=True)
    )


def gelu_parts(pre_act):
    cumul = 0.5 * (1.0 + jax.scipy.special.erf(pre_act * 0.7071067811865476))
    density = jnp.exp(-0.5 * pre_act * pre_act) * 0.3989422804014327
    return (pre_act * cumul, cumul + pre_act * density)


def shards(
    block_in,
    segment_ids,
    grad_out,
    qkv_weight,
    qv_bias,
    out_weight,
    up_weight,
    up_bias,
    down_weight,
    norm_gains,
    shift_biases,
):
    (
        query_key_value_full,
        qv_all,
        output_weight_full,
        up_weight_full,
        upbias_all,
        down_weight_full,
        gain_all,
        shift_all,
    ) = (
        lax.all_gather(qkv_weight, "shard", axis=0, tiled=True),
        lax.all_gather(qv_bias, "shard", axis=1, tiled=True),
        lax.all_gather(out_weight, "shard", axis=1, tiled=True),
        lax.all_gather(up_weight, "shard", axis=0, tiled=True),
        lax.all_gather(up_bias, "shard", axis=0, tiled=True),
        lax.all_gather(down_weight, "shard", axis=1, tiled=True),
        lax.all_gather(norm_gains, "shard", axis=1, tiled=True),
        lax.all_gather(shift_biases, "shard", axis=1, tiled=True),
    )
    seqs = block_in.shape[0]
    width = block_in.shape[2]
    length = segment_ids.shape[1]
    cols = query_key_value_full.shape[2]
    heads_here = cols // HEAD_DIM
    scale = 1.0 / math.sqrt(HEAD_DIM)
    gain_full = gain_all.astype(jnp.float32)
    shift_full = shift_all.astype(jnp.float32)
    qv_full = qv_all.astype(jnp.float32)
    inputs_bf = block_in.astype(jnp.bfloat16)
    input_rows_full = lax.all_gather(inputs_bf, "tensor", axis=1, tiled=True)
    query_key_value = jnp.einsum(
        "agp,pmy->agmy", input_rows_full, query_key_value_full, preferred_element_type=jnp.float32
    )
    query = (
        (query_key_value[:, :, 0] + qv_full[0])
        .astype(jnp.bfloat16)
        .reshape(seqs, length, heads_here, HEAD_DIM)
    )
    keys = query_key_value[:, :, 1].astype(jnp.bfloat16).reshape(seqs, length, heads_here, HEAD_DIM)
    values = (
        (query_key_value[:, :, 2] + qv_full[1])
        .astype(jnp.bfloat16)
        .reshape(seqs, length, heads_here, HEAD_DIM)
    )
    same = (segment_ids[:, :, None] == segment_ids[:, None, :])[:, None]
    scores = jnp.einsum("sqhe,skhe->shqk", query, keys, preferred_element_type=jnp.float32) * scale
    scores = jnp.where(same, scores, masked_score)
    highest = jnp.max(scores, axis=-1, keepdims=True)
    expo = jnp.exp(scores - highest)
    total = jnp.sum(expo, axis=-1, keepdims=True)
    probs = (expo / total).astype(jnp.bfloat16)
    log_total = highest + jnp.log(total)
    attention_context = jnp.einsum(
        "shqk,skhe->sqhe", probs, values, preferred_element_type=jnp.float32
    )
    attention_context = attention_context.astype(jnp.bfloat16).reshape(seqs, length, cols)
    attention_slice = jnp.einsum(
        "nip,pr->nir", attention_context, output_weight_full, preferred_element_type=jnp.float32
    )
    attended = lax.psum_scatter(attention_slice, "tensor", scatter_dimension=1, tiled=True)
    first_sum = block_in + (attended + shift_full[0])
    hidden, normed_one, inverse_one = norm_forward(first_sum, gain_full[0], shift_full[1])
    hidden_bf = hidden.astype(jnp.bfloat16)
    hidden_state_full = lax.all_gather(hidden_bf, "tensor", axis=1, tiled=True)
    pre_act = jnp.einsum(
        "peo,ot->pet", hidden_state_full, up_weight_full, preferred_element_type=jnp.float32
    ) + upbias_all.astype(jnp.float32)
    activ, slope = gelu_parts(pre_act)
    activation_bfloat = activ.astype(jnp.bfloat16)
    down_weight_slice = jnp.einsum(
        "uzt,tv->uzv", activation_bfloat, down_weight_full, preferred_element_type=jnp.float32
    )
    second_sum = hidden + (
        lax.psum_scatter(down_weight_slice, "tensor", scatter_dimension=1, tiled=True)
        + shift_full[2]
    )
    block_out, normed_two, inverse_two = norm_forward(second_sum, gain_full[1], shift_full[3])
    d_second = norm_backward(grad_out, normed_two, inverse_two, gain_full[1])
    second_gradient_full = lax.all_gather(
        d_second.astype(jnp.bfloat16), "tensor", axis=1, tiled=True
    )
    down_weight_gradient = jnp.einsum(
        "bct,bcm->tm", activation_bfloat, second_gradient_full, preferred_element_type=jnp.float32
    )
    d_pre = (
        jnp.einsum(
            "ajn,tn->ajt",
            second_gradient_full,
            down_weight_full,
            preferred_element_type=jnp.float32,
        )
        * slope
    )
    g_upbias = jnp.sum(d_pre, axis=(0, 1))
    preact_gradient_bfloat = d_pre.astype(jnp.bfloat16)
    up_weight_gradient = jnp.einsum(
        "ahk,ahp->kp", hidden_state_full, preact_gradient_bfloat, preferred_element_type=jnp.float32
    )
    hidden_state_slice = jnp.einsum(
        "ixj,gj->ixg", preact_gradient_bfloat, up_weight_full, preferred_element_type=jnp.float32
    )
    d_hidden = (
        lax.psum_scatter(hidden_state_slice, "tensor", scatter_dimension=1, tiled=True) + d_second
    )
    d_first = norm_backward(d_hidden, normed_one, inverse_one, gain_full[0])
    gain_part = jnp.stack(
        [jnp.sum(d_hidden * normed_one, axis=(0, 1)), jnp.sum(grad_out * normed_two, axis=(0, 1))]
    )
    shift_part = jnp.stack(
        [
            jnp.sum(d_first, axis=(0, 1)),
            jnp.sum(d_hidden, axis=(0, 1)),
            jnp.sum(d_second, axis=(0, 1)),
            jnp.sum(grad_out, axis=(0, 1)),
        ]
    )
    first_gradient_full = lax.all_gather(d_first.astype(jnp.bfloat16), "tensor", axis=1, tiled=True)
    output_weight_gradient = jnp.einsum(
        "unb,una->ba", attention_context, first_gradient_full, preferred_element_type=jnp.float32
    )
    context_gradient = jnp.einsum(
        "tbu,wu->tbw", first_gradient_full, output_weight_full, preferred_element_type=jnp.float32
    )
    context_gradient = context_gradient.astype(jnp.bfloat16).reshape(
        seqs, length, heads_here, HEAD_DIM
    )
    probs_back = jnp.exp(scores - log_total)
    d_probs = jnp.einsum(
        "sqhe,skhe->shqk", context_gradient, values, preferred_element_type=jnp.float32
    )
    row_dot = jnp.sum(probs_back * d_probs, axis=-1, keepdims=True)
    d_scores = (probs_back * (d_probs - row_dot)).astype(jnp.bfloat16)
    d_query = (
        jnp.einsum("shqk,skhe->sqhe", d_scores, keys, preferred_element_type=jnp.float32) * scale
    )
    d_keys = (
        jnp.einsum("shqk,sqhe->skhe", d_scores, query, preferred_element_type=jnp.float32) * scale
    )
    d_values = jnp.einsum(
        "shqk,sqhe->skhe",
        probs_back.astype(jnp.bfloat16),
        context_gradient,
        preferred_element_type=jnp.float32,
    )
    d_query = d_query.reshape(seqs, length, cols)
    d_keys = d_keys.reshape(seqs, length, cols)
    d_values = d_values.reshape(seqs, length, cols)
    g_qv = jnp.stack([jnp.sum(d_query, axis=(0, 1)), jnp.sum(d_values, axis=(0, 1))])
    projected_gradient_bfloat = jnp.stack([d_query, d_keys, d_values], axis=2).astype(jnp.bfloat16)
    projection_weight_gradient = jnp.einsum(
        "pjx,pjvy->xvy",
        input_rows_full,
        projected_gradient_bfloat,
        preferred_element_type=jnp.float32,
    )
    input_slice = jnp.einsum(
        "pxvk,yvk->pxy",
        projected_gradient_bfloat,
        query_key_value_full,
        preferred_element_type=jnp.float32,
    )
    grad_in = lax.psum_scatter(input_slice, "tensor", scatter_dimension=1, tiled=True) + d_first
    matrices = (
        projection_weight_gradient,
        output_weight_gradient,
        up_weight_gradient,
        down_weight_gradient,
    )
    spread = (
        lax.psum_scatter(matrices[0], ("shard", "replica"), scatter_dimension=0, tiled=True),
        lax.psum_scatter(matrices[1], ("shard", "replica"), scatter_dimension=1, tiled=True),
        lax.psum_scatter(matrices[2], ("shard", "replica"), scatter_dimension=0, tiled=True),
        lax.psum_scatter(matrices[3], ("shard", "replica"), scatter_dimension=1, tiled=True),
    )
    summed = (
        lax.all_gather(spread[0], "replica", axis=0, tiled=True),
        lax.all_gather(spread[1], "replica", axis=1, tiled=True),
        lax.all_gather(spread[2], "replica", axis=0, tiled=True),
        lax.all_gather(spread[3], "replica", axis=1, tiled=True),
    )
    tensor_index = lax.axis_index("tensor")
    shard_index = lax.axis_index("shard")
    shard_count = lax.axis_size("shard")
    tensor_count = lax.axis_size("tensor")
    upbias_width = upbias_all.shape[0]
    qv_wide = lax.dynamic_update_slice(
        jnp.zeros((2, width), jnp.float32), g_qv, (0, tensor_index * cols)
    )
    upbias_wide = lax.dynamic_update_slice(
        jnp.zeros((upbias_width * tensor_count,), jnp.float32),
        g_upbias,
        (tensor_index * upbias_width,),
    )
    gain_tot, shift_tot, qv_tot, upbias_tot = lax.psum(
        (gain_part, shift_part, qv_wide, upbias_wide), ("tensor", "shard", "replica")
    )
    vec_piece = norm_gains.shape[1]
    qv_piece = qv_bias.shape[1]
    upbias_piece = up_bias.shape[0]
    owner_index = tensor_index * shard_count + shard_index
    grad_gains = lax.dynamic_slice_in_dim(gain_tot, shard_index * vec_piece, vec_piece, 1)
    grad_shifts = lax.dynamic_slice_in_dim(shift_tot, shard_index * vec_piece, vec_piece, 1)
    grad_qv = lax.dynamic_slice_in_dim(qv_tot, owner_index * qv_piece, qv_piece, 1)
    grad_upbias = lax.dynamic_slice_in_dim(upbias_tot, owner_index * upbias_piece, upbias_piece, 0)
    return (
        block_out,
        grad_in,
        summed[0],
        grad_qv,
        summed[1],
        summed[2],
        grad_upbias,
        summed[3],
        grad_gains,
        grad_shifts,
    )


def solution(mesh):
    in_specs = (
        P(("shard", "replica"), "tensor", None),
        P(("shard", "replica"), None),
        P(("shard", "replica"), "tensor", None),
        P("shard", None, "tensor"),
        P(None, ("tensor", "shard")),
        P("tensor", "shard"),
        P("shard", "tensor"),
        P(("tensor", "shard")),
        P("tensor", "shard"),
        P(None, "shard"),
        P(None, "shard"),
    )
    out_specs = (
        P(("shard", "replica"), "tensor", None),
        P(("shard", "replica"), "tensor", None),
        P("shard", None, "tensor"),
        P(None, ("tensor", "shard")),
        P("tensor", "shard"),
        P("shard", "tensor"),
        P(("tensor", "shard")),
        P("tensor", "shard"),
        P(None, "shard"),
        P(None, "shard"),
    )
    return jax.shard_map(shards, mesh=mesh, in_specs=in_specs, out_specs=out_specs, check_vma=False)
```

profile of v0, /device:TPU:0, one launch (start us, length us, event | category | flops | bytes accessed | tf_op | source)
XLA Modules:
  0.0 765.2 jit_solution(3063412595622243338)
XLA Ops:
  10.6 5.2 all_gather.50
  16.0 11.6 %all_gather.51 = bf16[256,1024]{1,0:T(8,128)(2,1)S(1)} all-gather(bf16[256,512]{1,0:T(8,128)(2,1)S(1)} %copy-done.16), channel_id=1, replica_groups=mesh['tensor'=4,'shard'=2,'replica'=4] {'shard'}, dimensions={1}, use_global_device_ids=true | all-gather | bytes 786432 | tf_op jit(solution)/shard_map/all_gather | solution.py:62
  27.9 13.1 %all-gather.14.cloned.1.call-done = bf16[1024,3,256]{0,2,1:T(8,128)(2,1)} async-done(((bf16[512,3,256]{0,2,1:T(8,128)(2,1)}), bf16[1024,3,256]{0,2,1:T(8,128)(2,1)}) %all-gather.14.cloned.1.call-update) | async-done | bytes 1572880 | tf_op jit(solution)/shard_map/all_gather | solution.py:60
  40.9 36.2 %all-gather.12.cloned.1.call-done = bf16[1,640,1024]{2,1,0:T(8,128)(2,1)} async-done(((bf16[1,160,1024]{2,1,0:T(8,128)(2,1)}), bf16[1,640,1024]{2,1,0:T(8,128)(2,1)}) %all-gather.12.cloned.1.call-update) | async-done | bytes 1310736 | tf_op jit(solution)/shard_map/all_gather | solution.py:79
  88.6 4.4 all_gather.53
  93.0 4.3 all_gather.52
  97.4 42.1 %reduce-scatter.9.cloned.1.call-done = f32[1,160,1024]{2,1,0:T(8,128)} async-done(((f32[1,640,1024]{2,1,0:T(8,128)}), f32[1,160,1024]{2,1,0:T(8,128)}) %reduce-scatter.9.cloned.1.call-update) | async-done | bytes 655376 | tf_op jit(solution)/shard_map/reduce_scatter | solution.py:109
  142.6 4.4 all-gather
  146.9 26.6 %all-gather.18.cloned.1.call-done = bf16[1024,1024]{1,0:T(8,128)(2,1)} async-done(((bf16[512,1024]{1,0:T(8,128)(2,1)}), bf16[1024,1024]{1,0:T(8,128)(2,1)}) %all-gather.18.cloned.1.call-update) | async-done | bytes 2097168 | tf_op jit(solution)/shard_map/all_gather | solution.py:63
  173.6 34.5 %all-gather.16.cloned.1.call-done = bf16[1,640,1024]{2,1,0:T(8,128)(2,1)} async-done(((bf16[1,160,1024]{2,1,0:T(8,128)(2,1)}), bf16[1,640,1024]{2,1,0:T(8,128)(2,1)}) %all-gather.16.cloned.1.call-update) | async-done | bytes 1310736 | tf_op jit(solution)/shard_map/all_gather | solution.py:113
  208.1 5.1 multiply_convert_fusion.1
  213.2 28.5 %all-gather.20.cloned.1.call-done = bf16[1024,1024]{1,0:T(8,128)(2,1)} async-done(((bf16[1024,512]{1,0:T(8,128)(2,1)}), bf16[1024,1024]{1,0:T(8,128)(2,1)}) %all-gather.20.cloned.1.call-update) | async-done | bytes 2097168 | tf_op jit(solution)/shard_map/all_gather | solution.py:65
  241.7 4.6 convolution_bitcast_fusion.3
  246.4 52.4 %reduce-scatter.11.cloned.1.call-done = f32[1,160,1024]{2,1,0:T(8,128)} async-done(((f32[1,640,1024]{2,1,0:T(8,128)}), f32[1,160,1024]{2,1,0:T(8,128)}) %reduce-scatter.11.cloned.1.call-update) | async-done | bytes 655376 | tf_op jit(solution)/shard_map/reduce_scatter | solution.py:123
  303.0 32.0 %all-gather.22.cloned.1.call-done = bf16[1,640,1024]{2,1,0:T(8,128)(2,1)} async-done(((bf16[1,160,1024]{2,1,0:T(8,128)(2,1)}), bf16[1,640,1024]{2,1,0:T(8,128)(2,1)}) %all-gather.22.cloned.1.call-update) | async-done | bytes 1310736 | tf_op jit(solution)/shard_map/all_gather | solution.py:128
  335.0 5.3 fusion.49
  344.6 51.5 %reduce-scatter.13.cloned.1.call-done = f32[1,160,1024]{2,1,0:T(8,128)} async-done(((f32[1,640,1024]{2,1,0:T(8,128)}), f32[1,160,1024]{2,1,0:T(8,128)}) %reduce-scatter.13.cloned.1.call-update) | async-done | bytes 655376 | tf_op jit(solution)/shard_map/reduce_scatter | solution.py:152
  398.7 5.6 fusion.18
  405.7 5.2 fusion.15
  411.2 19.7 %all-gather.24.cloned.1.call-done = bf16[1,640,1024]{2,1,0:T(8,128)(2,1)} async-done(((bf16[1,160,1024]{2,1,0:T(8,128)(2,1)}), bf16[1,640,1024]{2,1,0:T(8,128)(2,1)}) %all-gather.24.cloned.1.call-update) | async-done | bytes 1310736 | tf_op jit(solution)/shard_map/all_gather | solution.py:166
  432.9 4.9 fusion.45
  439.9 5.6 multiply_reduce_fusion
  459.4 25.2 %reduce-scatter.21.cloned.1.call-done = f32[128,1024]{1,0:T(8,128)} async-done(((f32[1024,1024]{1,0:T(8,128)}), f32[128,1024]{1,0:T(8,128)}) %reduce-scatter.21.cloned.1.call-update) | async-done | bytes 524304 | tf_op jit(solution)/shard_map/reduce_scatter | solution.py:221
  484.6 54.2 %reduce-scatter.23.cloned.1.call-done = f32[1024,128]{1,0:T(8,128)} async-done(((f32[1024,1024]{1,0:T(8,128)}), f32[1024,128]{1,0:T(8,128)}) %reduce-scatter.23.cloned.1.call-update) | async-done | bytes 524304 | tf_op jit(solution)/shard_map/reduce_scatter | solution.py:222
  538.9 4.2 convolution_bitcast_fusion.1
  543.2 45.1 %reduce-scatter.17.cloned.1.call-done = f32[128,3,256]{0,2,1:T(8,128)} async-done(((f32[1024,3,256]{0,2,1:T(8,128)}), f32[128,3,256]{0,2,1:T(8,128)}) %reduce-scatter.17.cloned.1.call-update) | async-done | bytes 393232 | tf_op jit(solution)/shard_map/reduce_scatter | solution.py:219
  588.9 39.9 %all-reduce = (f32[2,1024]{1,0:T(2,128)S(1)}, f32[4096]{0:T(1024)S(1)}, f32[2,1024]{1,0:T(2,128)S(1)}, f32[4,1024]{1,0:T(4,128)S(1)}) all-reduce(f32[2,1024]{1,0:T(2,128)S(1)} %maximum_dynamic-update-slice_fusion, f32[4096]{0:T(1024)S(1)} %dynamic_update_slice.7, ...), channel_id=1, replica_groups=mesh['tensor'=4,'shard'=2,'replica'=4] {'tensor','shard','replica'}, use_global_device_ids=true, to_apply=%region_18.19 | all-reduce | flops 12288 | bytes 98304 | tf_op jit(solution)/shard_map/psum | solution.py:243
  631.2 8.1 %all_gather.61 = f32[256,512]{1,0:T(8,128)S(1)} all-gather(f32[256,128]{1,0:T(8,128)} %reduce-scatter.19.cloned.1.call-done), channel_id=1, replica_groups=mesh['tensor'=4,'shard'=2,'replica'=4] {'replica'}, dimensions={1}, use_global_device_ids=true | all-gather | bytes 655360 | tf_op jit(solution)/shard_map/all_gather | solution.py:226
  639.3 13.0 %all-gather.28.cloned.1.call-done = f32[512,1024]{1,0:T(8,128)} async-done(((f32[128,1024]{1,0:T(8,128)}), f32[512,1024]{1,0:T(8,128)}) %all-gather.28.cloned.1.call-update) | async-done | bytes 2097168 | tf_op jit(solution)/shard_map/all_gather | solution.py:227
  652.4 24.3 %all-gather.30.cloned.1.call-done = f32[1024,512]{1,0:T(8,128)} async-done(((f32[1024,128]{1,0:T(8,128)}), f32[1024,512]{1,0:T(8,128)}) %all-gather.30.cloned.1.call-update) | async-done | bytes 2097168 | tf_op jit(solution)/shard_map/all_gather | solution.py:228
  676.6 54.4 %reduce-scatter.15.cloned.1.call-done = f32[1,160,1024]{2,1,0:T(8,128)} async-done(((f32[1,640,1024]{2,1,0:T(8,128)}), f32[1,160,1024]{2,1,0:T(8,128)}) %reduce-scatter.15.cloned.1.call-update) | async-done | bytes 655376 | tf_op jit(solution)/shard_map/reduce_scatter | solution.py:211
  733.0 18.8 %all-gather.26.cloned.1.call-done = f32[512,3,256]{0,2,1:T(8,128)} async-done(((f32[128,3,256]{0,2,1:T(8,128)}), f32[512,3,256]{0,2,1:T(8,128)}) %all-gather.26.cloned.1.call-update) | async-done | bytes 1572880 | tf_op jit(solution)/shard_map/all_gather | solution.py:225
  (161 shorter events, 60.4 us)
Async XLA Ops:
  7.2 8.8 %copy-start.18 = (s32[1,640]{1,0:T(1,128)S(1)}, s32[1,640]{1,0:T(1,128)}, u32[]{:S(2)}) copy-start(s32[1,640]{1,0:T(1,128)} %param.12) | copy-start | bytes 7684
  7.2 8.8 %copy-start.16 = (bf16[256,512]{1,0:T(8,128)(2,1)S(1)}, bf16[256,512]{1,0:T(8,128)(2,1)}, u32[]{:S(2)}) copy-start(bf16[256,512]{1,0:T(8,128)(2,1)} %param.16) | copy-start | bytes 786436
  7.2 33.7 %all-gather.14.cloned.1.call-start = ((), (), s32[]{:S(2)}) async-start(), calls=%async_computation.9 | async-start | bytes 2359296 | tf_op jit(solution)/shard_map/all_gather | solution.py:60
  9.6 67.5 %all-gather.12.cloned.1.call-start = ((), (), s32[]{:S(2)}) async-start(), calls=%async_computation.8 | async-start | bytes 1638400 | tf_op jit(solution)/shard_map/all_gather | solution.py:79
  10.5 129.0 %reduce-scatter.9.cloned.1.call-start = ((), (), s32[]{:S(2)}) async-start(), calls=%async_computation.10 | async-start | bytes 3276800 | tf_op jit(solution)/shard_map/reduce_scatter | solution.py:109
  27.6 58.4 %copy-start.9 = (bf16[256,1024]{1,0:T(8,128)(2,1)}, bf16[256,1024]{1,0:T(8,128)(2,1)S(1)}, u32[]{:S(2)}) copy-start(bf16[256,1024]{1,0:T(8,128)(2,1)S(1)} %all_gather.51) | copy-start | bytes 1572868
  80.5 5.5 copy-start.4
  88.0 85.6 %all-gather.18.cloned.1.call-start = ((), (), s32[]{:S(2)}) async-start(), calls=%async_computation.12 | async-start | bytes 3145728 | tf_op jit(solution)/shard_map/all_gather | solution.py:63
  88.6 54.0 %copy-start.20 = (bf16[512]{0:T(512)(128)(2,1)S(1)}, bf16[512]{0:T(512)(128)(2,1)}, u32[]{:S(2)}) copy-start(bf16[512]{0:T(512)(128)(2,1)} %param.18) | copy-start | bytes 3076
  88.6 119.5 %all-gather.16.cloned.1.call-start = ((), (), s32[]{:S(2)}) async-start(), calls=%async_computation.11 | async-start | bytes 1638400 | tf_op jit(solution)/shard_map/all_gather | solution.py:113
  141.9 99.8 %all-gather.20.cloned.1.call-start = ((), (), s32[]{:S(2)}) async-start(), calls=%async_computation.13 | async-start | bytes 3145728 | tf_op jit(solution)/shard_map/all_gather | solution.py:65
  142.5 156.3 %reduce-scatter.11.cloned.1.call-start = ((), (), s32[]{:S(2)}) async-start(), calls=%async_computation.14 | async-start | bytes 3276800 | tf_op jit(solution)/shard_map/reduce_scatter | solution.py:123
  213.2 33.1 %copy-start.25 = (bf16[640,1024]{1,0:T(8,128)(2,1)}, bf16[640,1024]{1,0:T(8,128)(2,1)S(1)}, u32[]{:S(2)}) copy-start(bf16[640,1024]{1,0:T(8,128)(2,1)S(1)} %get-tuple-element.68) | copy-start | bytes 3932164
  246.4 54.1 %copy-start.6 = (f32[1,160,1024]{2,1,0:T(8,128)S(1)}, f32[1,160,1024]{2,1,0:T(8,128)}, u32[]{:S(2)}) copy-start(f32[1,160,1024]{2,1,0:T(8,128)} %param.13) | copy-start | bytes 1966084
  246.4 88.6 %all-gather.22.cloned.1.call-start = ((), (), s32[]{:S(2)}) async-start(), calls=%async_computation.15 | async-start | bytes 1638400 | tf_op jit(solution)/shard_map/all_gather | solution.py:128
  302.8 93.3 %reduce-scatter.13.cloned.1.call-start = ((), (), s32[]{:S(2)}) async-start(), calls=%async_computation.16 | async-start | bytes 3276800 | tf_op jit(solution)/shard_map/reduce_scatter | solution.py:152
  335.0 6.3 copy-start.21
  344.5 86.4 %all-gather.24.cloned.1.call-start = ((), (), s32[]{:S(2)}) async-start(), calls=%async_computation.17 | async-start | bytes 1638400 | tf_op jit(solution)/shard_map/all_gather | solution.py:166
  397.8 6.5 copy-start.2
  398.7 85.9 %reduce-scatter.21.cloned.1.call-start = ((), (), s32[]{:S(2)}) async-start(), calls=%async_computation.22 | async-start | bytes 4718592 | tf_op jit(solution)/shard_map/reduce_scatter | solution.py:221
  404.4 134.5 %reduce-scatter.23.cloned.1.call-start = ((), (), s32[]{:S(2)}) async-start(), calls=%async_computation.24 | async-start | bytes 4718592 | tf_op jit(solution)/shard_map/reduce_scatter | solution.py:222
  410.9 20.0 %copy-start.10 = (bf16[256,1024]{1,0:T(8,128)(2,1)S(1)}, bf16[256,1024]{1,0:T(8,128)(2,1)}, u32[]{:S(2)}) copy-start(bf16[256,1024]{1,0:T(8,128)(2,1)} %copy-done.9) | copy-start | bytes 1572868
  410.9 177.4 %reduce-scatter.17.cloned.1.call-start = ((), (), s32[]{:S(2)}) async-start(), calls=%async_computation.19 | async-start | bytes 3538944 | tf_op jit(solution)/shard_map/reduce_scatter | solution.py:219
  437.8 7.7 %slice-start = ((s8[6553600]{0:T(1024)(128)(4,1)}), s8[2359296]{0:T(1024)(128)(4,1)S(1)}, s32[]{:S(2)}) async-start(s8[6553600]{0:T(1024)(128)(4,1)} %bitcast.97), calls=%async_computation.26 | async-start | bytes 4718592
  439.9 5.6 slice-start.1
  456.4 174.8 %reduce-scatter.19.cloned.1.call-start = ((), (), s32[]{:S(2)}) async-start(), calls=%async_computation.21 | async-start | bytes 1179648 | tf_op jit(solution)/shard_map/reduce_scatter | solution.py:220
  459.3 193.0 %all-gather.28.cloned.1.call-start = ((), (), s32[]{:S(2)}) async-start(), calls=%async_computation.23 | async-start | bytes 2621440 | tf_op jit(solution)/shard_map/all_gather | solution.py:227
  484.6 192.0 %all-gather.30.cloned.1.call-start = ((), (), s32[]{:S(2)}) async-start(), calls=%async_computation.25 | async-start | bytes 2621440 | tf_op jit(solution)/shard_map/all_gather | solution.py:228
  538.9 192.1 %reduce-scatter.15.cloned.1.call-start = ((), (), s32[]{:S(2)}) async-start(), calls=%async_computation.18 | async-start | bytes 3276800 | tf_op jit(solution)/shard_map/reduce_scatter | solution.py:211
  543.1 187.9 %copy-start.3 = (f32[1,160,1024]{2,1,0:T(8,128)S(1)}, f32[1,160,1024]{2,1,0:T(8,128)}, u32[]{:S(2)}) copy-start(f32[1,160,1024]{2,1,0:T(8,128)} %copy-done.2) | copy-start | bytes 1966084
  543.1 208.7 %all-gather.26.cloned.1.call-start = ((), (), s32[]{:S(2)}) async-start(), calls=%async_computation.20 | async-start | bytes 1966080 | tf_op jit(solution)/shard_map/all_gather | solution.py:225
  652.4 103.3 %copy-start.7 = (f32[512,1024]{1,0:T(8,128)S(1)}, f32[512,1024]{1,0:T(8,128)}, u32[]{:S(2)}) copy-start(f32[512,1024]{1,0:T(8,128)} %all-gather.28.cloned.1.call-done) | copy-start | bytes 6291460
  (15 other events, 37.2 us)
Sparse Core Ops, SparseCore 0:
  10.1 30.7 all-gather.13
  43.1 33.9 all-gather.11
  88.1 51.3 reduce-scatter.8
  140.9 32.6 all-gather.17
  175.5 32.5 all-gather.15
  209.5 32.1 all-gather.19
  246.5 52.2 reduce-scatter.10
  302.9 32.0 all-gather.21
  344.6 51.3 reduce-scatter.12
  398.8 32.0 all-gather.23
  434.3 50.2 reduce-scatter.20
  487.8 51.0 reduce-scatter.22
  542.3 46.0 reduce-scatter.16
  591.9 36.2 reduce-scatter.18
  629.6 22.6 all-gather.27
  653.8 22.8 all-gather.29
  678.8 52.2 reduce-scatter.14
  732.5 19.3 all-gather.25
where the time goes:
time: 766 us; the launch traced here: 765 us
  waiting for transfers between devices  573 us (75%)
  blocking collectives  77.8 us (10%)
  matrix products  62.1 us (8%)
  local copies, waits for them, and re-layouts  21.9 us (3%)
  between operations  14.8 us (2%)
  other arithmetic  14.5 us (2%)
    reduce_scatter x1, waiting for transfers between devices, shards(): lax.psum_scatter(input_slice, 'tensor', scatter_dimension=1, tiled=True)  54.4 us
    reduce_scatter x1, waiting for transfers between devices, shards(): lax.psum_scatter(matrices[3], ('shard', 'replica'), scatter_dimension=1,...  54.2 us
    reduce_scatter x1, waiting for transfers between devices, shards(): lax.psum_scatter(down_weight_slice, 'tensor', scatter_dimension=1, tiled=...  52.4 us
    reduce_scatter x1, waiting for transfers between devices, shards(): lax.psum_scatter(hidden_state_slice, 'tensor', scatter_dimension=1, tiled...  51.5 us
    reduce_scatter x1, waiting for transfers between devices, shards(): lax.psum_scatter(matrices[0], ('shard', 'replica'), scatter_dimension=0,...  45.1 us
    reduce_scatter x1, waiting for transfers between devices, shards(): lax.psum_scatter(attention_slice, 'tensor', scatter_dimension=1, tiled=True)  42.1 us
    psum x1, blocking collectives, shards(): lax.psum((gain_part, shift_part, qv_wide, upbias_wide), ('tensor', 'shard...  39.9 us
    all_gather x1, waiting for transfers between devices, shards(): input_rows_full = lax.all_gather(inputs_bf, 'tensor', axis=1, tiled=True)  36.2 us
  transfers between devices with their start and end apart: 18, of which 17 were waited for; matrix products, arithmetic and copies ran while one was open for 7% of the time, Pallas kernels for 0%

commit v1 on v0

--- a/solution.py
+++ b/solution.py
@@ -32,6 +32,12 @@
     cumul = 0.5 * (1.0 + jax.scipy.special.erf(pre_act * 0.7071067811865476))
     density = jnp.exp(-0.5 * pre_act * pre_act) * 0.3989422804014327
     return (pre_act * cumul, cumul + pre_act * density)
+
+
+def scatter_sum(part, axes, dim):
+    return lax.psum_scatter(
+        part.astype(jnp.bfloat16), axes, scatter_dimension=dim, tiled=True
+    )
 
 
 def shards(
@@ -47,6 +53,19 @@
     norm_gains,
     shift_biases,
 ):
+    small = (qv_bias, up_bias[None], norm_gains, shift_biases)
+    packed = lax.all_gather(
+        jnp.concatenate([vec.reshape(-1) for vec in small]), "shard", axis=0
+    )
+    unpacked = []
+    start = 0
+    for vec in small:
+        rows, piece = vec.shape
+        part = packed[:, start : start + rows * piece].reshape(-1, rows, piece)
+        unpacked.append(jnp.swapaxes(part, 0, 1).reshape(rows, -1))
+        start += rows * piece
+    qv_packed, upbias_packed, gain_packed, shift_packed = unpacked
+    upbias_packed = upbias_packed[0]
     (
         query_key_value_full,
         qv_all,
@@ -58,13 +77,13 @@
         shift_all,
     ) = (
         lax.all_gather(qkv_weight, "shard", axis=0, tiled=True),
-        lax.all_gather(qv_bias, "shard", axis=1, tiled=True),
+        qv_packed,
         lax.all_gather(out_weight, "shard", axis=1, tiled=True),
         lax.all_gather(up_weight, "shard", axis=0, tiled=True),
-        lax.all_gather(up_bias, "shard", axis=0, tiled=True),
+        upbias_packed,
         lax.all_gather(down_weight, "shard", axis=1, tiled=True),
-        lax.all_gather(norm_gains, "shard", axis=1, tiled=True),
-        lax.all_gather(shift_biases, "shard", axis=1, tiled=True),
+        gain_packed,
+        shift_packed,
     )
     seqs = block_in.shape[0]
     width = block_in.shape[2]
@@ -106,7 +125,7 @@
     attention_slice = jnp.einsum(
         "nip,pr->nir", attention_context, output_weight_full, preferred_element_type=jnp.float32
     )
-    attended = lax.psum_scatter(attention_slice, "tensor", scatter_dimension=1, tiled=True)
+    attended = scatter_sum(attention_slice, "tensor", 1).astype(jnp.float32)
     first_sum = block_in + (attended + shift_full[0])
     hidden, normed_one, inverse_one = norm_forward(first_sum, gain_full[0], shift_full[1])
     hidden_bf = hidden.astype(jnp.bfloat16)
@@ -120,7 +139,7 @@
         "uzt,tv->uzv", activation_bfloat, down_weight_full, preferred_element_type=jnp.float32
     )
     second_sum = hidden + (
-        lax.psum_scatter(down_weight_slice, "tensor", scatter_dimension=1, tiled=True)
+        scatter_sum(down_weight_slice, "tensor", 1).astype(jnp.float32)
         + shift_full[2]
     )
     block_out, normed_two, inverse_two = norm_forward(second_sum, gain_full[1], shift_full[3])
@@ -149,7 +168,7 @@
         "ixj,gj->ixg", preact_gradient_bfloat, up_weight_full, preferred_element_type=jnp.float32
     )
     d_hidden = (
-        lax.psum_scatter(hidden_state_slice, "tensor", scatter_dimension=1, tiled=True) + d_second
+        scatter_sum(hidden_state_slice, "tensor", 1).astype(jnp.float32) + d_second
     )
     d_first = norm_backward(d_hidden, normed_one, inverse_one, gain_full[0])
     gain_part = jnp.stack(
@@ -208,7 +227,7 @@
         query_key_value_full,
         preferred_element_type=jnp.float32,
     )
-    grad_in = lax.psum_scatter(input_slice, "tensor", scatter_dimension=1, tiled=True) + d_first
+    grad_in = scatter_sum(input_slice, "tensor", 1).astype(jnp.float32) + d_first
     matrices = (
         projection_weight_gradient,
         output_weight_gradient,
@@ -216,16 +235,16 @@
         down_weight_gradient,
     )
     spread = (
-        lax.psum_scatter(matrices[0], ("shard", "replica"), scatter_dimension=0, tiled=True),
-        lax.psum_scatter(matrices[1], ("shard", "replica"), scatter_dimension=1, tiled=True),
-        lax.psum_scatter(matrices[2], ("shard", "replica"), scatter_dimension=0, tiled=True),
-        lax.psum_scatter(matrices[3], ("shard", "replica"), scatter_dimension=1, tiled=True),
+        scatter_sum(matrices[0], ("shard", "replica"), 0),
+        scatter_sum(matrices[1], ("shard", "replica"), 1),
+        scatter_sum(matrices[2], ("shard", "replica"), 0),
+        scatter_sum(matrices[3], ("shard", "replica"), 1),
     )
     summed = (
-        lax.all_gather(spread[0], "replica", axis=0, tiled=True),
-        lax.all_gather(spread[1], "replica", axis=1, tiled=True),
-        lax.all_gather(spread[2], "replica", axis=0, tiled=True),
-        lax.all_gather(spread[3], "replica", axis=1, tiled=True),
+        lax.all_gather(spread[0], "replica", axis=0, tiled=True).astype(jnp.float32),
+        lax.all_gather(spread[1], "replica", axis=1, tiled=True).astype(jnp.float32),
+        lax.all_gather(spread[2], "replica", axis=0, tiled=True).astype(jnp.float32),
+        lax.all_gather(spread[3], "replica", axis=1, tiled=True).astype(jnp.float32),
     )
     tensor_index = lax.axis_index("tensor")
     shard_index = lax.axis_index("shard")

time: 766 us -> 612 us (0.80)
  waiting for transfers between devices: 573 us -> 412 us
  other arithmetic: 14.5 us -> 27.4 us
    reduce_scatter x8 -> x5, waiting for transfers between devices: 325 us -> 141 us  [scatter_sum(): lax.psum_scatter(part.astype(jnp.bfloat16), axes, scatter_dimension=dim,...]
    unnamed x18 -> x20, waiting for transfers between devices: 1.31 us -> 65.7 us
    all_gather x3 -> x2, waiting for transfers between devices: 56.1 us -> 0.01 us  [the longest x1 0.01 us: shards(): lax.all_gather(spread[2], 'replica', axis=0, tiled=True).astype(jnp.float32)]
    all_gather x1, waiting for transfers between devices: 19.7 us -> 32.7 us  [shards(): lax.all_gather(d_first.astype(jnp.bfloat16), 'tensor', axis=1, tiled=True)]
    all_gather x5 -> x3, blocking collectives: 26.4 us -> 20.4 us  [the longest x1 8.59 us: shards(): lax.all_gather(spread[0], 'replica', axis=0, tiled=True).astype(jnp.float32)]
    unnamed x64 -> x93, local copies, waits for them, and re-layouts: 16.2 us -> 17.3 us
  transfers between devices with their start and end apart: 18 -> 17, of which waited for: 17 -> 14; matrix products, arithmetic and copies ran while one was open for 7% -> 13% of each run, Pallas kernels for 0% -> 0%
where the time goes in v1:
time: 612 us; the launch traced here: 611 us
  waiting for transfers between devices  412 us (67%)
  blocking collectives  72.4 us (12%)
  matrix products  58.1 us (9%)
  other arithmetic  27.4 us (4%)
  local copies, waits for them, and re-layouts  25.5 us (4%)
  between operations  14.7 us (2%)
    reduce_scatter x5, waiting for transfers between devices, scatter_sum(): lax.psum_scatter(part.astype(jnp.bfloat16), axes, scatter_dimension=dim,...  141 us
    unnamed x20, waiting for transfers between devices  65.7 us
    psum x1, blocking collectives, shards(): lax.psum((gain_part, shift_part, qv_wide, upbias_wide), ('tensor', 'shard...  40 us
    all_gather x1, waiting for transfers between devices, shards(): input_rows_full = lax.all_gather(inputs_bf, 'tensor', axis=1, tiled=True)  36.2 us
    all_gather x1, waiting for transfers between devices, shards(): hidden_state_full = lax.all_gather(hidden_bf, 'tensor', axis=1, tiled=True)  34.5 us
    all_gather x1, waiting for transfers between devices, shards(): lax.all_gather(d_first.astype(jnp.bfloat16), 'tensor', axis=1, tiled=True)  32.7 us
    all_gather x1, waiting for transfers between devices, shards(): lax.all_gather(d_second.astype(jnp.bfloat16), 'tensor', axis=1, tiled=True)  31.1 us
    all_gather x1, waiting for transfers between devices, shards(): lax.all_gather(up_weight, 'shard', axis=0, tiled=True)  30.2 us
  transfers between devices with their start and end apart: 17, of which 14 were waited for; matrix products, arithmetic and copies ran while one was open for 13% of the time, Pallas kernels for 0%

profile of v1, /device:TPU:0, one launch (start us, length us, event | category | flops | bytes accessed | tf_op | source)
XLA Modules:
  0.0 611.5 jit_solution(1188588645892185024)
XLA Ops:
  10.7 5.4 all-gather.1
  16.3 12.0 %all_gather.46 = bf16[256,1024]{1,0:T(8,128)(2,1)S(1)} all-gather(bf16[256,512]{1,0:T(8,128)(2,1)S(1)} %copy-done.16), channel_id=1, replica_groups=mesh['tensor'=4,'shard'=2,'replica'=4] {'shard'}, dimensions={1}, use_global_device_ids=true | all-gather | bytes 786432 | tf_op jit(solution)/shard_map/all_gather | solution.py:81
  28.6 12.7 %all-gather.14.cloned.1.call-done = bf16[1024,3,256]{0,2,1:T(8,128)(2,1)} async-done(((bf16[512,3,256]{0,2,1:T(8,128)(2,1)}), bf16[1024,3,256]{0,2,1:T(8,128)(2,1)}) %all-gather.14.cloned.1.call-update) | async-done | bytes 1572880 | tf_op jit(solution)/shard_map/all_gather | solution.py:79
  41.3 36.2 %all-gather.12.cloned.1.call-done = bf16[1,640,1024]{2,1,0:T(8,128)(2,1)} async-done(((bf16[1,160,1024]{2,1,0:T(8,128)(2,1)}), bf16[1,640,1024]{2,1,0:T(8,128)(2,1)}) %all-gather.12.cloned.1.call-update) | async-done | bytes 1310736 | tf_op jit(solution)/shard_map/all_gather | solution.py:98
  77.4 3.2 convolution_bitcast_fusion
  89.4 29.9 %reduce-scatter.15.cloned.1.call-done = bf16[1,160,1024]{2,1,0:T(8,128)(2,1)} async-done(((bf16[1,640,1024]{2,1,0:T(8,128)(2,1)}), bf16[1,160,1024]{2,1,0:T(8,128)(2,1)}) %reduce-scatter.15.cloned.1.call-update) | async-done | bytes 327696 | tf_op jit(solution)/shard_map/reduce_scatter | solution.py:38
  122.2 30.2 %all-gather.18.cloned.1.call-done = bf16[1024,1024]{1,0:T(8,128)(2,1)} async-done(((bf16[512,1024]{1,0:T(8,128)(2,1)}), bf16[1024,1024]{1,0:T(8,128)(2,1)}) %all-gather.18.cloned.1.call-update) | async-done | bytes 2097168 | tf_op jit(solution)/shard_map/all_gather | solution.py:82
  152.4 34.5 %all-gather.16.cloned.1.call-done = bf16[1,640,1024]{2,1,0:T(8,128)(2,1)} async-done(((bf16[1,160,1024]{2,1,0:T(8,128)(2,1)}), bf16[1,640,1024]{2,1,0:T(8,128)(2,1)}) %all-gather.16.cloned.1.call-update) | async-done | bytes 1310736 | tf_op jit(solution)/shard_map/all_gather | solution.py:132
  187.0 5.2 multiply_convert_fusion.1
  192.2 28.4 %all-gather.20.cloned.1.call-done = bf16[1024,1024]{1,0:T(8,128)(2,1)} async-done(((bf16[1024,512]{1,0:T(8,128)(2,1)}), bf16[1024,1024]{1,0:T(8,128)(2,1)}) %all-gather.20.cloned.1.call-update) | async-done | bytes 2097168 | tf_op jit(solution)/shard_map/all_gather | solution.py:84
  220.6 4.2 fusion.12
  224.9 31.5 %reduce-scatter.17.cloned.1.call-done = bf16[1,160,1024]{2,1,0:T(8,128)(2,1)} async-done(((bf16[1,640,1024]{2,1,0:T(8,128)(2,1)}), bf16[1,160,1024]{2,1,0:T(8,128)(2,1)}) %reduce-scatter.17.cloned.1.call-update) | async-done | bytes 327696 | tf_op jit(solution)/shard_map/reduce_scatter | solution.py:38
  260.2 31.1 %all-gather.22.cloned.1.call-done = bf16[1,640,1024]{2,1,0:T(8,128)(2,1)} async-done(((bf16[1,160,1024]{2,1,0:T(8,128)(2,1)}), bf16[1,640,1024]{2,1,0:T(8,128)(2,1)}) %all-gather.22.cloned.1.call-update) | async-done | bytes 1310736 | tf_op jit(solution)/shard_map/all_gather | solution.py:147
  291.4 5.9 fusion.55
  301.0 4.9 convolution_convert_fusion.1
  305.9 3.6 convolution_convert_fusion
  312.2 19.4 %reduce-scatter.19.cloned.1.call-done = bf16[1,160,1024]{2,1,0:T(8,128)(2,1)} async-done(((bf16[1,640,1024]{2,1,0:T(8,128)(2,1)}), bf16[1,160,1024]{2,1,0:T(8,128)(2,1)}) %reduce-scatter.19.cloned.1.call-update) | async-done | bytes 327696 | tf_op jit(solution)/shard_map/reduce_scatter | solution.py:38
  337.4 37.6 %reduce-scatter.23.cloned.1.call-done = bf16[128,1024]{1,0:T(8,128)(2,1)} async-done(((bf16[1024,1024]{1,0:T(8,128)(2,1)}), bf16[128,1024]{1,0:T(8,128)(2,1)}) %reduce-scatter.23.cloned.1.call-update) | async-done | bytes 262160 | tf_op jit(solution)/shard_map/reduce_scatter | solution.py:38
  375.2 44.9 %reduce-scatter.29.cloned.1.call-done = bf16[128,1024]{1,0:T(8,128)(2,1)} async-done(((bf16[1024,1024]{1,0:T(8,128)(2,1)}), bf16[128,1024]{1,0:T(8,128)(2,1)}) %reduce-scatter.29.cloned.1.call-update) | async-done | bytes 262160
  422.0 32.7 %all-gather.24.cloned.1.call-done = bf16[1,640,1024]{2,1,0:T(8,128)(2,1)} async-done(((bf16[1,160,1024]{2,1,0:T(8,128)(2,1)}), bf16[1,640,1024]{2,1,0:T(8,128)(2,1)}) %all-gather.24.cloned.1.call-update) | async-done | bytes 1310736 | tf_op jit(solution)/shard_map/all_gather | solution.py:185
  459.8 5.0 fusion.51
  464.8 4.0 multiply_reduce_fusion
  469.2 6.0 multiply_convert_fusion
  480.4 3.1 fusion.33
  484.6 3.0 convolution_convert_fusion.2
  489.3 3.7 fusion.11
  493.6 40.0 %all-reduce = (f32[2,1024]{1,0:T(2,128)S(1)}, f32[4096]{0:T(1024)S(1)}, f32[2,1024]{1,0:T(2,128)S(1)}, f32[4,1024]{1,0:T(4,128)S(1)}) all-reduce(f32[2,1024]{1,0:T(2,128)S(1)} %maximum_dynamic-update-slice_fusion, f32[4096]{0:T(1024)S(1)} %dynamic_update_slice.7, ...), channel_id=1, replica_groups=mesh['tensor'=4,'shard'=2,'replica'=4] {'tensor','shard','replica'}, use_global_device_ids=true, to_apply=%region_18.19 | all-reduce | flops 12288 | bytes 98304 | tf_op jit(solution)/shard_map/psum | solution.py:262
  538.8 2.9 convert_element_type.225
  542.7 6.5 %all_gather.53 = bf16[256,512]{1,0:T(8,128)(2,1)S(1)} all-gather(bf16[256,128]{1,0:T(8,128)(2,1)S(1)} %copy.63), channel_id=1, replica_groups=mesh['tensor'=4,'shard'=2,'replica'=4] {'replica'}, dimensions={1}, use_global_device_ids=true | all-gather | bytes 327680 | tf_op jit(solution)/shard_map/all_gather | solution.py:245
  550.0 19.5 %reduce-scatter.25.cloned.1.call-done = bf16[128,768]{1,0:T(8,128)(2,1)} async-done(((bf16[1024,768]{1,0:T(8,128)(2,1)}), bf16[128,768]{1,0:T(8,128)(2,1)}) %reduce-scatter.25.cloned.1.call-update) | async-done | bytes 196624
  570.6 8.6 %all_gather.52 = bf16[512,3,256]{0,2,1:T(8,128)(2,1)S(1)} all-gather(bf16[128,3,256]{0,2,1:T(8,128)(2,1)S(1)} %bitcast.140), channel_id=1, replica_groups=mesh['tensor'=4,'shard'=2,'replica'=4] {'replica'}, dimensions={0}, use_global_device_ids=true | all-gather | bytes 983040 | tf_op jit(solution)/shard_map/all_gather | solution.py:244
  580.6 22.5 %reduce-scatter.21.cloned.1.call-done = bf16[1,160,1024]{2,1,0:T(8,128)(2,1)} async-done(((bf16[1,640,1024]{2,1,0:T(8,128)(2,1)}), bf16[1,160,1024]{2,1,0:T(8,128)(2,1)}) %reduce-scatter.21.cloned.1.call-update) | async-done | bytes 327696 | tf_op jit(solution)/shard_map/reduce_scatter | solution.py:38
  (193 shorter events, 58.7 us)
Async XLA Ops:
  7.2 9.1 %copy-start.31 = (s32[1,640]{1,0:T(1,128)S(1)}, s32[1,640]{1,0:T(1,128)}, u32[]{:S(2)}) copy-start(s32[1,640]{1,0:T(1,128)} %param.12) | copy-start | bytes 7684
  7.2 9.1 %copy-start.16 = (bf16[256,512]{1,0:T(8,128)(2,1)S(1)}, bf16[256,512]{1,0:T(8,128)(2,1)}, u32[]{:S(2)}) copy-start(bf16[256,512]{1,0:T(8,128)(2,1)} %param.16) | copy-start | bytes 786436
  7.2 34.0 %all-gather.14.cloned.1.call-start = ((), (), s32[]{:S(2)}) async-start(), calls=%async_computation.9 | async-start | bytes 2359296 | tf_op jit(solution)/shard_map/all_gather | solution.py:79
  9.7 67.8 %all-gather.12.cloned.1.call-start = ((), (), s32[]{:S(2)}) async-start(), calls=%async_computation.8 | async-start | bytes 1638400 | tf_op jit(solution)/shard_map/all_gather | solution.py:98
  10.5 108.7 %reduce-scatter.15.cloned.1.call-start = ((), (), s32[]{:S(2)}) async-start(), calls=%async_computation.10 | async-start | bytes 1638400 | tf_op jit(solution)/shard_map/reduce_scatter | solution.py:38
  16.2 66.9 %copy-start.27 = (f32[4,64]{1,0:T(4,128)}, f32[4,64]{1,0:T(4,128)S(1)}, u32[]{:S(2)}) copy-start(f32[4,64]{1,0:T(4,128)S(1)} %add.169) | copy-start | bytes 3076
  28.3 58.0 %copy-start.11 = (bf16[256,1024]{1,0:T(8,128)(2,1)}, bf16[256,1024]{1,0:T(8,128)(2,1)S(1)}, u32[]{:S(2)}) copy-start(bf16[256,1024]{1,0:T(8,128)(2,1)S(1)} %all_gather.46) | copy-start | bytes 1572868
  88.6 63.8 %all-gather.18.cloned.1.call-start = ((), (), s32[]{:S(2)}) async-start(), calls=%async_computation.12 | async-start | bytes 3145728 | tf_op jit(solution)/shard_map/all_gather | solution.py:82
  89.2 97.8 %all-gather.16.cloned.1.call-start = ((), (), s32[]{:S(2)}) async-start(), calls=%async_computation.11 | async-start | bytes 1638400 | tf_op jit(solution)/shard_map/all_gather | solution.py:132
  121.6 99.1 %all-gather.20.cloned.1.call-start = ((), (), s32[]{:S(2)}) async-start(), calls=%async_computation.13 | async-start | bytes 3145728 | tf_op jit(solution)/shard_map/all_gather | solution.py:84
  122.1 134.2 %reduce-scatter.17.cloned.1.call-start = ((), (), s32[]{:S(2)}) async-start(), calls=%async_computation.14 | async-start | bytes 1638400 | tf_op jit(solution)/shard_map/reduce_scatter | solution.py:38
  192.2 28.4 %copy-start.36 = (bf16[640,1024]{1,0:T(8,128)(2,1)}, bf16[640,1024]{1,0:T(8,128)(2,1)S(1)}, u32[]{:S(2)}) copy-start(bf16[640,1024]{1,0:T(8,128)(2,1)S(1)} %get-tuple-element.78) | copy-start | bytes 3932164
  224.8 33.1 %copy-start.10 = (f32[1,160,1024]{2,1,0:T(8,128)S(1)}, f32[1,160,1024]{2,1,0:T(8,128)}, u32[]{:S(2)}) copy-start(f32[1,160,1024]{2,1,0:T(8,128)} %param.13) | copy-start | bytes 1966084
  224.8 66.5 %all-gather.22.cloned.1.call-start = ((), (), s32[]{:S(2)}) async-start(), calls=%async_computation.15 | async-start | bytes 1638400 | tf_op jit(solution)/shard_map/all_gather | solution.py:147
  260.0 71.6 %copy-start.4 = (f32[1,160,1024]{2,1,0:T(8,128)}, f32[1,160,1024]{2,1,0:T(8,128)S(1)}, u32[]{:S(2)}) copy-start(f32[1,160,1024]{2,1,0:T(8,128)S(1)} %get-tuple-element.58) | copy-start | bytes 1966084
  260.0 71.6 %reduce-scatter.19.cloned.1.call-start = ((), (), s32[]{:S(2)}) async-start(), calls=%async_computation.16 | async-start | bytes 1638400 | tf_op jit(solution)/shard_map/reduce_scatter | solution.py:38
  291.4 6.9 %copy-start.35 = (bf16[1024,1024]{1,0:T(8,128)(2,1)S(1)}, bf16[1024,1024]{1,0:T(8,128)(2,1)}, u32[]{:S(2)}) copy-start(bf16[1024,1024]{1,0:T(8,128)(2,1)} %all-gather.18.cloned.1.call-done) | copy-start | bytes 6291460
  300.9 74.1 %reduce-scatter.23.cloned.1.call-start = ((), (), s32[]{:S(2)}) async-start(), calls=%async_computation.19 | async-start | bytes 2359296 | tf_op jit(solution)/shard_map/reduce_scatter | solution.py:38
  305.9 114.2 %reduce-scatter.29.cloned.1.call-start = ((), (), s32[]{:S(2)}) async-start(), calls=%async_computation.24 | async-start | bytes 2359296
  312.1 142.5 %all-gather.24.cloned.1.call-start = ((), (), s32[]{:S(2)}) async-start(), calls=%async_computation.17 | async-start | bytes 1638400 | tf_op jit(solution)/shard_map/all_gather | solution.py:185
  333.6 131.2 %slice-start = ((s8[6553600]{0:T(1024)(128)(4,1)}), s8[2359296]{0:T(1024)(128)(4,1)S(1)}, s32[]{:S(2)}) async-start(s8[6553600]{0:T(1024)(128)(4,1)} %bitcast.122), calls=%async_computation.25 | async-start | bytes 4718592
  335.8 86.2 %copy-start.18 = (f32[4,640]{1,0:T(4,128)S(1)}, f32[4,640]{1,0:T(4,128)}, u32[]{:S(2)}) copy-start(f32[4,640]{1,0:T(4,128)} %copy-done.17) | copy-start | bytes 30724
  335.8 86.2 %copy-start.20 = (f32[4,640]{1,0:T(4,128)S(1)}, f32[4,640]{1,0:T(4,128)}, u32[]{:S(2)}) copy-start(f32[4,640]{1,0:T(4,128)} %copy-done.19) | copy-start | bytes 30724
  337.4 198.6 %all-gather.26.cloned.1.call-start = ((), (), s32[]{:S(2)}) async-start(), calls=%async_computation.20 | async-start | bytes 1310720 | tf_op jit(solution)/shard_map/all_gather | solution.py:246
  375.1 82.6 %copy-start.12 = (bf16[256,1024]{1,0:T(8,128)(2,1)S(1)}, bf16[256,1024]{1,0:T(8,128)(2,1)}, u32[]{:S(2)}) copy-start(bf16[256,1024]{1,0:T(8,128)(2,1)} %copy-done.11) | copy-start | bytes 1572868
  375.1 163.7 %all-gather.28.cloned.1.call-start = ((), (), s32[]{:S(2)}) async-start(), calls=%async_computation.21 | async-start | bytes 1310720 | tf_op jit(solution)/shard_map/all_gather | solution.py:247
  421.9 119.8 %reduce-scatter.27.cloned.1.call-start = ((), (), s32[]{:S(2)}) async-start(), calls=%async_computation.23 | async-start | bytes 589824
  457.7 7.1 %slice-start.1 = ((s8[6553600]{0:T(1024)(128)(4,1)}), s8[4194304]{0:T(1024)(128)(4,1)S(1)}, s32[]{:S(2)}) async-start(s8[6553600]{0:T(1024)(128)(4,1)} %bitcast.122), calls=%async_computation.26 | async-start | bytes 8388608
  468.9 100.6 %reduce-scatter.25.cloned.1.call-start = ((), (), s32[]{:S(2)}) async-start(), calls=%async_computation.22 | async-start | bytes 1769472
  469.2 6.0 copy-start.6
  489.2 113.8 %reduce-scatter.21.cloned.1.call-start = ((), (), s32[]{:S(2)}) async-start(), calls=%async_computation.18 | async-start | bytes 1638400 | tf_op jit(solution)/shard_map/reduce_scatter | solution.py:38
  549.1 53.9 %copy-start.3 = (f32[1,160,1024]{2,1,0:T(8,128)S(1)}, f32[1,160,1024]{2,1,0:T(8,128)}, u32[]{:S(2)}) copy-start(f32[1,160,1024]{2,1,0:T(8,128)} %copy-done.2) | copy-start | bytes 1966084
  (25 other events, 74.9 us)
Sparse Core Ops, SparseCore 0:
  10.2 31.0 all-gather.13
  43.4 33.9 all-gather.11
  88.7 30.4 reduce-scatter.14
  120.6 31.7 all-gather.17
  154.4 32.5 all-gather.15
  188.4 32.1 all-gather.19
  224.9 31.3 reduce-scatter.16
  260.1 31.1 all-gather.21
  301.1 30.4 reduce-scatter.18
  335.3 39.7 reduce-scatter.22
  378.9 41.1 reduce-scatter.28
  422.1 32.5 all-gather.23
  456.2 15.7 all-gather.25
  473.5 16.8 all-gather.27
  493.2 34.1 reduce-scatter.26
  531.1 38.3 reduce-scatter.24
  571.6 31.3 reduce-scatter.20

commit v2 on v1

--- a/solution.py
+++ b/solution.py
@@ -1,8 +1,11 @@
+import functools
 import math
 
 import jax
 import jax.numpy as jnp
 from jax import lax
+from jax.experimental import pallas as pl
+from jax.experimental.pallas import tpu as pltpu
 from jax.sharding import PartitionSpec as P
 
 HEAD_DIM = 64
@@ -38,6 +41,327 @@
     return lax.psum_scatter(
         part.astype(jnp.bfloat16), axes, scatter_dimension=dim, tiled=True
     )
+
+
+def remote(src, dst, send, recv, where):
+    return pltpu.make_async_remote_copy(
+        src_ref=src,
+        dst_ref=dst,
+        send_sem=send,
+        recv_sem=recv,
+        device_id=where,
+        device_id_type=pl.DeviceIdType.MESH,
+    )
+
+
+def greet(peers):
+    barrier = pltpu.get_barrier_semaphore()
+    for where in peers:
+        pl.semaphore_signal(
+            barrier, inc=1, device_id=where, device_id_type=pl.DeviceIdType.MESH
+        )
+    pl.semaphore_wait(barrier, len(peers))
+
+
+def block_of(ref, kind, shape, piece, half):
+    rows, cols = shape
+    depth = rows // 2
+    if kind == 0:
+        return ref.at[pl.ds(pl.multiple_of(piece * rows + half * depth, depth), depth), :]
+    return ref.at[
+        pl.ds(pl.multiple_of(half * depth, depth), depth),
+        pl.ds(pl.multiple_of(piece * cols, cols), cols),
+    ]
+
+
+def gather_kernel(n, kinds, shapes, *refs):
+    count = len(kinds)
+    ins, outs = refs[:count], refs[count : 2 * count]
+    local, far_send, far_recv, near_send, near_recv = refs[2 * count :]
+    me = lax.axis_index("shard")
+    rep = lax.axis_index("replica")
+    core = lax.rem(rep, 2)
+    partner = {"replica": rep + 1 - 2 * core}
+    greet([{"shard": lax.rem(me + k, n)} for k in range(1, n)] + [partner])
+    far, near = {}, {}
+    for i in range(count):
+        for k in range(1, n):
+            where = {"shard": lax.rem(me + k, n)}
+            if kinds[i] == 2:
+                src, dst = ins[i], outs[i].at[me]
+            else:
+                depth = shapes[i][0] // 2
+                src = ins[i].at[pl.ds(pl.multiple_of(core * depth, depth), depth), :]
+                dst = block_of(outs[i], kinds[i], shapes[i], me, core)
+            far[i, k] = remote(src, dst, far_send.at[i, k - 1], far_recv.at[i, k - 1], where)
+            far[i, k].start()
+    own = []
+    for i in range(count):
+        rows, cols = shapes[i]
+        if kinds[i] == 2:
+            dst = outs[i].at[me]
+        elif kinds[i] == 0:
+            dst = outs[i].at[pl.ds(pl.multiple_of(me * rows, rows), rows), :]
+        else:
+            dst = outs[i].at[:, pl.ds(pl.multiple_of(me * cols, cols), cols)]
+        own.append(pltpu.make_async_copy(ins[i], dst, local.at[i]))
+        own[-1].start()
+    for i in range(count):
+        for k in range(1, n):
+            far[i, k].wait_recv()
+            if kinds[i] != 2:
+                block = block_of(outs[i], kinds[i], shapes[i], lax.rem(me + n - k, n), core)
+                near[i, k] = remote(
+                    block, block, near_send.at[i, k - 1], near_recv.at[i, k - 1], partner
+                )
+                near[i, k].start()
+    for copy in near.values():
+        copy.wait()
+    for copy in far.values():
+        copy.wait_send()
+    for copy in own:
+        copy.wait()
+
+
+def gather_blocks(arrays, kinds, ident):
+    n = lax.axis_size("shard")
+    shapes = [a.shape for a in arrays]
+    out = []
+    for a, kind in zip(arrays, kinds):
+        rows, cols = a.shape
+        full = ((n * rows, cols), (rows, n * cols), (n, rows, cols))[kind]
+        out.append(jax.ShapeDtypeStruct(full, a.dtype))
+    vmem = pl.BlockSpec(memory_space=pltpu.VMEM)
+    grid = (len(arrays), max(n - 1, 1))
+    total = sum(a.size * a.dtype.itemsize for a in arrays) * n
+    return pl.pallas_call(
+        functools.partial(gather_kernel, n, kinds, shapes),
+        out_shape=out,
+        in_specs=[vmem] * len(arrays),
+        out_specs=[vmem] * len(arrays),
+        scratch_shapes=[pltpu.SemaphoreType.DMA((len(arrays),))]
+        + [pltpu.SemaphoreType.DMA(grid)] * 4,
+        cost_estimate=pl.CostEstimate(
+            flops=0, bytes_accessed=20 * total, transcendentals=0
+        ),
+        compiler_params=pltpu.CompilerParams(collective_id=ident, has_side_effects=True),
+    )(*arrays)
+
+
+def row_loop(rows, body):
+    step = min(rows, 32)
+
+    @pl.loop(0, rows // step)
+    def _(j):
+        body(pl.ds(pl.multiple_of(j * step, step), step))
+
+
+def grad_kernel(n, m, kinds, *refs):
+    count = len(kinds)
+    ins, outs = refs[:count], refs[count : 2 * count]
+    got, half, pieces, slots = (refs[(2 + q) * count : (3 + q) * count] for q in range(4))
+    a_send, a_recv, b_send, b_recv, c_send, c_recv, d_send, d_recv = refs[6 * count :]
+    me = lax.axis_index("shard")
+    rep = lax.axis_index("replica")
+    core = lax.rem(rep, 2)
+    chips = m // 2
+    chip = rep // 2
+    partner = {"replica": rep + 1 - 2 * core}
+    shard_peers = [{"shard": lax.rem(me + k, n)} for k in range(1, n)]
+    chip_peers = [{"replica": lax.rem(chip + k, chips) * 2 + core} for k in range(1, chips)]
+    greet([partner] + shard_peers + chip_peers)
+    f32 = jnp.float32
+    first, second, third, fourth = [], {}, {}, []
+
+    def piece_of(i, index):
+        if kinds[i] == 0:
+            return half[i].at[index]
+        cols = outs[i].shape[2]
+        return half[i].at[:, pl.ds(pl.multiple_of(index * cols, cols), cols)]
+
+    for i in range(count):
+        src = ins[i].at[:, 1 - core] if kinds[i] == 0 else ins[i].at[1 - core]
+        first.append(remote(src, got[i], a_send.at[i], a_recv.at[i], partner))
+        first[i].start()
+    for i in range(count):
+        first[i].wait_recv()
+        rows = outs[i].shape[1]
+        if kinds[i] == 0:
+
+            @pl.loop(0, n)
+            def _(p):
+                def add(at):
+                    half[i][p, at] = (
+                        ins[i][p, core, at].astype(f32) + got[i][p, at].astype(f32)
+                    ).astype(jnp.bfloat16)
+
+                row_loop(rows, add)
+
+        else:
+
+            def add(at):
+                half[i][at] = (
+                    ins[i][core, at].astype(f32) + got[i][at].astype(f32)
+                ).astype(jnp.bfloat16)
+
+            row_loop(rows, add)
+        for k in range(1, n):
+            second[i, k] = remote(
+                piece_of(i, lax.rem(me + k, n)),
+                pieces[i].at[k - 1],
+                b_send.at[i, k - 1],
+                b_recv.at[i, k - 1],
+                shard_peers[k - 1],
+            )
+            second[i, k].start()
+    for i in range(count):
+        for k in range(1, n):
+            second[i, k].wait_recv()
+        mine = piece_of(i, me)
+
+        def add_pieces(at):
+            total = mine[at].astype(f32)
+            for k in range(1, n):
+                total = total + pieces[i][k - 1, at].astype(f32)
+            slots[i][chip, at] = total.astype(jnp.bfloat16)
+
+        row_loop(outs[i].shape[1], add_pieces)
+        for k in range(1, chips):
+            third[i, k] = remote(
+                slots[i].at[chip],
+                slots[i].at[chip],
+                c_send.at[i, k - 1],
+                c_recv.at[i, k - 1],
+                chip_peers[k - 1],
+            )
+            third[i, k].start()
+    for i in range(count):
+        for k in range(1, chips):
+            third[i, k].wait_recv()
+
+        def add_chips(at):
+            total = slots[i][0, at].astype(f32)
+            for q in range(1, chips):
+                total = total + slots[i][q, at].astype(f32)
+            outs[i][core, at] = total.astype(jnp.bfloat16)
+
+        row_loop(outs[i].shape[1], add_chips)
+        fourth.append(
+            remote(outs[i].at[core], outs[i].at[core], d_send.at[i], d_recv.at[i], partner)
+        )
+        fourth[i].start()
+    for copy in fourth:
+        copy.wait()
+    for copy in first + list(second.values()) + list(third.values()):
+        copy.wait_send()
+
+
+def sum_grads(grads, kinds, ident):
+    n, m = lax.axis_size("shard"), lax.axis_size("replica")
+    bf = jnp.bfloat16
+    views, out, got, pieces, slots = [], [], [], [], []
+    for g, kind in zip(grads, kinds):
+        rows, cols = g.shape
+        if kind == 0:
+            deep, wide = rows // (2 * n), cols
+            views.append(g.reshape(n, 2, deep, cols))
+            got.append((n, deep, cols))
+        else:
+            deep, wide = rows // 2, cols // n
+            views.append(g.reshape(2, deep, cols))
+            got.append((deep, cols))
+        out.append(jax.ShapeDtypeStruct((2, deep, wide), bf))
+        pieces.append((max(n - 1, 1), deep, wide))
+        slots.append((m // 2, deep, wide))
+    count = len(grads)
+    vmem = pl.BlockSpec(memory_space=pltpu.VMEM)
+    one = pltpu.SemaphoreType.DMA((count,))
+    by_shard = pltpu.SemaphoreType.DMA((count, max(n - 1, 1)))
+    by_chip = pltpu.SemaphoreType.DMA((count, max(m // 2 - 1, 1)))
+    total = sum(g.size * 2 for g in grads)
+    res = pl.pallas_call(
+        functools.partial(grad_kernel, n, m, kinds),
+        out_shape=out,
+        in_specs=[vmem] * count,
+        out_specs=[vmem] * count,
+        scratch_shapes=[pltpu.VMEM(t, bf) for t in got + got + pieces + slots]
+        + [one, one, by_shard, by_shard, by_chip, by_chip, one, one],
+        cost_estimate=pl.CostEstimate(
+            flops=0, bytes_accessed=30 * total, transcendentals=0
+        ),
+        compiler_params=pltpu.CompilerParams(collective_id=ident, has_side_effects=True),
+    )(*views)
+    return [r.reshape(-1, r.shape[2]).astype(jnp.float32) for r in res]
+
+
+def small_kernel(sizes, shared, local, out, *scratch):
+    slots, send, recv = scratch[0:3], scratch[3:6], scratch[6:9]
+    names = ("tensor", "replica", "shard")
+    here = [lax.axis_index(name) for name in names]
+    greet(
+        [
+            {names[a]: lax.rem(here[a] + k, sizes[a])}
+            for a in range(3)
+            for k in range(1, sizes[a])
+        ]
+    )
+    deep = shared.shape[0]
+    for a in range(3):
+        if a == 0:
+            slots[0][here[0]] = shared[...]
+        copies = [
+            remote(
+                shared if a == 0 else slots[a].at[here[a]],
+                slots[a].at[here[a]],
+                send[a].at[k - 1],
+                recv[a].at[k - 1],
+                {names[a]: lax.rem(here[a] + k, sizes[a])},
+            )
+            for k in range(1, sizes[a])
+        ]
+        for copy in copies:
+            copy.start()
+        for copy in copies:
+            copy.wait_recv()
+        total = slots[a][0]
+        for k in range(1, sizes[a]):
+            total = total + slots[a][k]
+        if a == 0:
+            slots[1][here[1], 0:deep] = total
+            slots[1][here[1], deep:] = local[...]
+        elif a == 1:
+            slots[2][here[2]] = total
+        else:
+            out[...] = total
+        for copy in copies:
+            copy.wait_send()
+
+
+def as_rows(vec):
+    flat = vec.reshape(-1)
+    return jnp.pad(flat, (0, -flat.shape[0] % 1024)).reshape(-1, 128)
+
+
+def sum_small(shared, local, ident):
+    sizes = tuple(lax.axis_size(a) for a in ("tensor", "replica", "shard"))
+    deep, low = shared.shape[0], local.shape[0]
+    vmem = pl.BlockSpec(memory_space=pltpu.VMEM)
+    sems = [pltpu.SemaphoreType.DMA((max(k - 1, 1),)) for k in sizes]
+    return pl.pallas_call(
+        functools.partial(small_kernel, sizes),
+        out_shape=jax.ShapeDtypeStruct((deep + low, 128), jnp.float32),
+        in_specs=[vmem] * 2,
+        out_specs=vmem,
+        scratch_shapes=[
+            pltpu.VMEM((sizes[0], deep, 128), jnp.float32),
+            pltpu.VMEM((sizes[1], deep + low, 128), jnp.float32),
+            pltpu.VMEM((sizes[2], deep + low, 128), jnp.float32),
+        ]
+        + sems
+        + sems,
+        cost_estimate=pl.CostEstimate(flops=0, bytes_accessed=20000000, transcendentals=0),
+        compiler_params=pltpu.CompilerParams(collective_id=ident, has_side_effects=True),
+    )(shared, local)
 
 
 def shards(
@@ -54,9 +378,21 @@
     shift_biases,
 ):
     small = (qv_bias, up_bias[None], norm_gains, shift_biases)
-    packed = lax.all_gather(
-        jnp.concatenate([vec.reshape(-1) for vec in small]), "shard", axis=0
-    )
+    inputs_bf = block_in.astype(jnp.bfloat16)
+    input_rows_full = lax.all_gather(inputs_bf, "tensor", axis=1, tiled=True)
+    cols = qkv_weight.shape[2]
+    query_key_value_full, output_weight_full, packed = gather_blocks(
+        (
+            qkv_weight.reshape(-1, 3 * cols),
+            out_weight,
+            as_rows(
+                jnp.concatenate([vec.reshape(-1) for vec in small]).astype(jnp.float32)
+            ),
+        ),
+        (0, 1, 2),
+        1,
+    )
+    packed = packed.reshape(packed.shape[0], -1)
     unpacked = []
     start = 0
     for vec in small:
@@ -64,52 +400,23 @@
         part = packed[:, start : start + rows * piece].reshape(-1, rows, piece)
         unpacked.append(jnp.swapaxes(part, 0, 1).reshape(rows, -1))
         start += rows * piece
-    qv_packed, upbias_packed, gain_packed, shift_packed = unpacked
-    upbias_packed = upbias_packed[0]
-    (
-        query_key_value_full,
-        qv_all,
-        output_weight_full,
-        up_weight_full,
-        upbias_all,
-        down_weight_full,
-        gain_all,
-        shift_all,
-    ) = (
-        lax.all_gather(qkv_weight, "shard", axis=0, tiled=True),
-        qv_packed,
-        lax.all_gather(out_weight, "shard", axis=1, tiled=True),
-        lax.all_gather(up_weight, "shard", axis=0, tiled=True),
-        upbias_packed,
-        lax.all_gather(down_weight, "shard", axis=1, tiled=True),
-        gain_packed,
-        shift_packed,
-    )
+    qv_all, upbias_all, gain_all, shift_all = unpacked
+    upbias_all = upbias_all[0]
     seqs = block_in.shape[0]
     width = block_in.shape[2]
     length = segment_ids.shape[1]
-    cols = query_key_value_full.shape[2]
     heads_here = cols // HEAD_DIM
     scale = 1.0 / math.sqrt(HEAD_DIM)
     gain_full = gain_all.astype(jnp.float32)
     shift_full = shift_all.astype(jnp.float32)
     qv_full = qv_all.astype(jnp.float32)
-    inputs_bf = block_in.astype(jnp.bfloat16)
-    input_rows_full = lax.all_gather(inputs_bf, "tensor", axis=1, tiled=True)
     query_key_value = jnp.einsum(
-        "agp,pmy->agmy", input_rows_full, query_key_value_full, preferred_element_type=jnp.float32
-    )
-    query = (
-        (query_key_value[:, :, 0] + qv_full[0])
-        .astype(jnp.bfloat16)
-        .reshape(seqs, length, heads_here, HEAD_DIM)
-    )
-    keys = query_key_value[:, :, 1].astype(jnp.bfloat16).reshape(seqs, length, heads_here, HEAD_DIM)
-    values = (
-        (query_key_value[:, :, 2] + qv_full[1])
-        .astype(jnp.bfloat16)
-        .reshape(seqs, length, heads_here, HEAD_DIM)
-    )
+        "agp,pm->agm", input_rows_full, query_key_value_full, preferred_element_type=jnp.float32
+    )
+    split = (seqs, length, heads_here, HEAD_DIM)
+    query = (query_key_value[:, :, :cols] + qv_full[0]).astype(jnp.bfloat16).reshape(split)
+    keys = query_key_value[:, :, cols : 2 * cols].astype(jnp.bfloat16).reshape(split)
+    values = (query_key_value[:, :, 2 * cols :] + qv_full[1]).astype(jnp.bfloat16).reshape(split)
     same = (segment_ids[:, :, None] == segment_ids[:, None, :])[:, None]
     scores = jnp.einsum("sqhe,skhe->shqk", query, keys, preferred_element_type=jnp.float32) * scale
     scores = jnp.where(same, scores, masked_score)
@@ -125,6 +432,10 @@
     attention_slice = jnp.einsum(
         "nip,pr->nir", attention_context, output_weight_full, preferred_element_type=jnp.float32
     )
+    up_weight, down_weight, attention_slice = lax.optimization_barrier(
+        (up_weight, down_weight, attention_slice)
+    )
+    up_weight_full, down_weight_full = gather_blocks((up_weight, down_weight), (0, 1), 2)
     attended = scatter_sum(attention_slice, "tensor", 1).astype(jnp.float32)
     first_sum = block_in + (attended + shift_full[0])
     hidden, normed_one, inverse_one = norm_forward(first_sum, gain_full[0], shift_full[1])
@@ -214,71 +525,52 @@
     d_keys = d_keys.reshape(seqs, length, cols)
     d_values = d_values.reshape(seqs, length, cols)
     g_qv = jnp.stack([jnp.sum(d_query, axis=(0, 1)), jnp.sum(d_values, axis=(0, 1))])
-    projected_gradient_bfloat = jnp.stack([d_query, d_keys, d_values], axis=2).astype(jnp.bfloat16)
+    projected_gradient_bfloat = jnp.concatenate([d_query, d_keys, d_values], axis=2).astype(jnp.bfloat16)
     projection_weight_gradient = jnp.einsum(
-        "pjx,pjvy->xvy",
+        "pjx,pjv->xv",
         input_rows_full,
         projected_gradient_bfloat,
         preferred_element_type=jnp.float32,
     )
     input_slice = jnp.einsum(
-        "pxvk,yvk->pxy",
+        "pxv,yv->pxy",
         projected_gradient_bfloat,
         query_key_value_full,
         preferred_element_type=jnp.float32,
     )
     grad_in = scatter_sum(input_slice, "tensor", 1).astype(jnp.float32) + d_first
-    matrices = (
-        projection_weight_gradient,
-        output_weight_gradient,
-        up_weight_gradient,
-        down_weight_gradient,
-    )
-    spread = (
-        scatter_sum(matrices[0], ("shard", "replica"), 0),
-        scatter_sum(matrices[1], ("shard", "replica"), 1),
-        scatter_sum(matrices[2], ("shard", "replica"), 0),
-        scatter_sum(matrices[3], ("shard", "replica"), 1),
-    )
-    summed = (
-        lax.all_gather(spread[0], "replica", axis=0, tiled=True).astype(jnp.float32),
-        lax.all_gather(spread[1], "replica", axis=1, tiled=True).astype(jnp.float32),
-        lax.all_gather(spread[2], "replica", axis=0, tiled=True).astype(jnp.float32),
-        lax.all_gather(spread[3], "replica", axis=1, tiled=True).astype(jnp.float32),
-    )
-    tensor_index = lax.axis_index("tensor")
+    bf = jnp.bfloat16
+    grad_up, grad_down = sum_grads(
+        (up_weight_gradient.astype(bf), down_weight_gradient.astype(bf)), (0, 1), 3
+    )
+    grad_qkv_flat, grad_out_weight = sum_grads(
+        (projection_weight_gradient.astype(bf), output_weight_gradient.astype(bf)), (0, 1), 4
+    )
+    grad_qkv = grad_qkv_flat.reshape(-1, 3, cols)
     shard_index = lax.axis_index("shard")
-    shard_count = lax.axis_size("shard")
-    tensor_count = lax.axis_size("tensor")
-    upbias_width = upbias_all.shape[0]
-    qv_wide = lax.dynamic_update_slice(
-        jnp.zeros((2, width), jnp.float32), g_qv, (0, tensor_index * cols)
-    )
-    upbias_wide = lax.dynamic_update_slice(
-        jnp.zeros((upbias_width * tensor_count,), jnp.float32),
-        g_upbias,
-        (tensor_index * upbias_width,),
-    )
-    gain_tot, shift_tot, qv_tot, upbias_tot = lax.psum(
-        (gain_part, shift_part, qv_wide, upbias_wide), ("tensor", "shard", "replica")
-    )
+    shared = as_rows(jnp.concatenate([gain_part, shift_part]))
+    sums = sum_small(shared, as_rows(jnp.concatenate([g_qv.reshape(-1), g_upbias])), 5)
+    wide = sums[: shared.shape[0]].reshape(-1)[: 6 * width].reshape(6, width)
+    gain_tot, shift_tot = wide[:2], wide[2:]
+    own = sums[shared.shape[0] :].reshape(-1)
+    qv_tot = own[: 2 * cols].reshape(2, cols)
+    upbias_tot = own[2 * cols : 2 * cols + g_upbias.shape[0]]
     vec_piece = norm_gains.shape[1]
     qv_piece = qv_bias.shape[1]
     upbias_piece = up_bias.shape[0]
-    owner_index = tensor_index * shard_count + shard_index
     grad_gains = lax.dynamic_slice_in_dim(gain_tot, shard_index * vec_piece, vec_piece, 1)
     grad_shifts = lax.dynamic_slice_in_dim(shift_tot, shard_index * vec_piece, vec_piece, 1)
-    grad_qv = lax.dynamic_slice_in_dim(qv_tot, owner_index * qv_piece, qv_piece, 1)
-    grad_upbias = lax.dynamic_slice_in_dim(upbias_tot, owner_index * upbias_piece, upbias_piece, 0)
+    grad_qv = lax.dynamic_slice_in_dim(qv_tot, shard_index * qv_piece, qv_piece, 1)
+    grad_upbias = lax.dynamic_slice_in_dim(upbias_tot, shard_index * upbias_piece, upbias_piece, 0)
     return (
         block_out,
         grad_in,
-        summed[0],
+        grad_qkv,
         grad_qv,
-        summed[1],
-        summed[2],
+        grad_out_weight,
+        grad_up,
         grad_upbias,
-        summed[3],
+        grad_down,
         grad_gains,
         grad_shifts,
     )

time: 612 us -> 416 us (0.68)
  waiting for transfers between devices: 412 us -> 166 us
  Pallas kernels: 0 us -> 141 us
  blocking collectives: 72.4 us -> 0 us
  local copies, waits for them, and re-layouts: 25.5 us -> 18.7 us
    pallas_call x0 -> x5, Pallas kernels: none -> 141 us  [the longest x2 78.3 us: sum_grads(): pl.pallas_call(functools.partial(grad_kernel, n, m, kinds), out_shape=out...]
    all_gather x5 -> x0, waiting for transfers between devices: 71.4 us -> none  [the longest x1 30.2 us: shards(): lax.all_gather(up_weight, 'shard', axis=0, tiled=True)]
    unnamed x20 -> x8, waiting for transfers between devices: 65.7 us -> 0.13 us
    reduce_scatter x5 -> x4, waiting for transfers between devices: 141 us -> 91.6 us  [scatter_sum(): lax.psum_scatter(part.astype(jnp.bfloat16), axes, scatter_dimension=dim,...]
    psum x1 -> x0, blocking collectives: 40 us -> none  [shards(): lax.psum((gain_part, shift_part, qv_wide, upbias_wide), ('tensor', 'shard...]
    all_gather x1, waiting for transfers between devices: 34.5 us -> 0.74 us  [shards(): hidden_state_full = lax.all_gather(hidden_bf, 'tensor', axis=1, tiled=True)]
    all_gather x4 -> x0, blocking collectives: 32.4 us -> none  [the longest x1 12 us: shards(): lax.all_gather(out_weight, 'shard', axis=1, tiled=True)]
    all_gather x1, waiting for transfers between devices: 36.2 us -> 11.1 us  [shards(): input_rows_full = lax.all_gather(inputs_bf, 'tensor', axis=1, tiled=True)]
  transfers between devices with their start and end apart: 17 -> 8, of which waited for: 14 -> 7; matrix products, arithmetic and copies ran while one was open for 13% -> 8% of each run, Pallas kernels for 0% -> 34%
where the time goes in v2:
time: 416 us; the launch traced here: 415 us
  waiting for transfers between devices  166 us (40%)
  Pallas kernels  141 us (34%)
  matrix products  52.1 us (13%)
  other arithmetic  22 us (5%)
  local copies, waits for them, and re-layouts  18.7 us (4%)
  between operations  14.7 us (4%)
    reduce_scatter x4, waiting for transfers between devices, scatter_sum(): lax.psum_scatter(part.astype(jnp.bfloat16), axes, scatter_dimension=dim,...  91.6 us
    pallas_call x2, Pallas kernels, sum_grads(): pl.pallas_call(functools.partial(grad_kernel, n, m, kinds), out_shape=out...  78.3 us
    pallas_call x2, Pallas kernels, gather_blocks(): pl.pallas_call(functools.partial(gather_kernel, n, kinds, shapes), out_sh...  50 us
    all_gather x1, waiting for transfers between devices, shards(): lax.all_gather(d_first.astype(jnp.bfloat16), 'tensor', axis=1, tiled=True)  31.3 us
    all_gather x1, waiting for transfers between devices, shards(): lax.all_gather(d_second.astype(jnp.bfloat16), 'tensor', axis=1, tiled=True)  31.1 us
    pallas_call x1, Pallas kernels, sum_small(): pl.pallas_call(functools.partial(small_kernel, sizes), out_shape=jax.Shap...  12.8 us
    all_gather x1, waiting for transfers between devices, shards(): input_rows_full = lax.all_gather(inputs_bf, 'tensor', axis=1, tiled=True)  11.1 us
    unnamed x64, local copies, waits for them, and re-layouts  10 us
  transfers between devices with their start and end apart: 8, of which 7 were waited for; matrix products, arithmetic and copies ran while one was open for 8% of the time, Pallas kernels for 34%

profile of v2, /device:TPU:0, one launch (start us, length us, event | category | flops | bytes accessed | tf_op | source)
XLA Modules:
  0.0 415.1 jit_solution(5311611160744915774)
XLA Ops:
  7.2 1.9 convert_element_type.135
  13.8 19.4 %shard_map.186 = (bf16[1024,768]{1,0:T(8,128)(2,1)}, bf16[256,1024]{1,0:T(8,128)(2,1)}, f32[2,32,128]{2,1,0:T(8,128)}) custom-call(bf16[512,768]{1,0:T(8,128)(2,1)} %copy.29.refs_0_, bf16[256,512]{1,0:T(8,128)(2,1)} %refs_1_.1, f32[32,128]{1,0:T(8,128)} %fusion.51.refs_2_), custom_call_target="tpu_custom_call" | custom-call | bytes 42598400 | tf_op jit(solution)/shard_map/pallas_call | solution.py:137
  34.3 11.1 %all-gather.5.cloned.1.call-done = bf16[1,640,1024]{2,1,0:T(8,128)(2,1)} async-done(((bf16[1,160,1024]{2,1,0:T(8,128)(2,1)}), bf16[1,640,1024]{2,1,0:T(8,128)(2,1)}) %all-gather.5.cloned.1.call-update) | async-done | bytes 1310736 | tf_op jit(solution)/shard_map/all_gather | solution.py:382
  45.4 3.2 convolution_bitcast_fusion.1
  51.1 1.8 copy-done
  54.3 1.6 convolution_bitcast_fusion
  56.1 30.5 %reduce-scatter.5.cloned.1.call-done = bf16[1,160,1024]{2,1,0:T(8,128)(2,1)} async-done(((bf16[1,640,1024]{2,1,0:T(8,128)(2,1)}), bf16[1,160,1024]{2,1,0:T(8,128)(2,1)}) %reduce-scatter.5.cloned.1.call-update) | async-done | bytes 327696 | tf_op jit(solution)/shard_map/reduce_scatter | solution.py:41
  88.9 30.5 %shard_map.187 = (bf16[1024,1024]{1,0:T(8,128)(2,1)}, bf16[1024,1024]{1,0:T(8,128)(2,1)}) custom-call(bf16[512,1024]{1,0:T(8,128)(2,1)} %refs_0_, bf16[1024,512]{1,0:T(8,128)(2,1)} %refs_1_.2), custom_call_target="tpu_custom_call" | custom-call | bytes 83886080 | tf_op jit(solution)/shard_map/pallas_call | solution.py:137
  120.2 5.3 %multiply_convert_fusion.1 = (bf16[640,1024]{1,0:T(8,128)(2,1)S(1)}, f32[640,1024]{1,0:T(8,128)}) fusion(f32[1024]{0:T(1024)S(1)} %bitcast.199, bf16[1024,1024]{1,0:T(8,128)(2,1)} %get-tuple-element.28, bf16[1,640,1024]{2,1,0:T(8,128)(2,1)} %all-gather.7.cloned.1.call-done), kind=kOutput, calls=%fused_computation.17 | convolution fusion | flops 1346109440 | bytes 7344128 | tf_op jit(solution)/shard_map/peo,ot->pet/dot_general | solution.py:444
  126.7 2.6 fusion.13
  129.4 30.6 %reduce-scatter.7.cloned.1.call-done = bf16[1,160,1024]{2,1,0:T(8,128)(2,1)} async-done(((bf16[1,640,1024]{2,1,0:T(8,128)(2,1)}), bf16[1,160,1024]{2,1,0:T(8,128)(2,1)}) %reduce-scatter.7.cloned.1.call-update) | async-done | bytes 327696 | tf_op jit(solution)/shard_map/reduce_scatter | solution.py:41
  163.3 31.1 %all-gather.9.cloned.1.call-done = bf16[1,640,1024]{2,1,0:T(8,128)(2,1)} async-done(((bf16[1,160,1024]{2,1,0:T(8,128)(2,1)}), bf16[1,640,1024]{2,1,0:T(8,128)(2,1)}) %all-gather.9.cloned.1.call-update) | async-done | bytes 1310736 | tf_op jit(solution)/shard_map/all_gather | solution.py:458
  194.5 5.3 %fusion.66 = (f32[1024]{0:T(1024)S(1)}, bf16[640,1024]{1,0:T(8,128)(2,1)S(1)}) fusion(f32[640,1024]{1,0:T(8,128)} %get-tuple-element.89, f32[1024]{0:T(1024)S(1)} %bitcast.200, bf16[1024,1024]{1,0:T(8,128)(2,1)} %get-tuple-element.29, bf16[1,640,1024]{2,1,0:T(8,128)(2,1)} %all-gather.9.cloned.1.call-done), kind=kOutput, calls=%fused_computation.123 | convolution fusion | flops 1350040576 | bytes 7348224 | tf_op jit(solution)/shard_map/ajn,tn->ajt/dot_general | solution.py:465
  200.8 2.6 fusion.14
  203.5 30.6 %reduce-scatter.9.cloned.1.call-done = bf16[1,160,1024]{2,1,0:T(8,128)(2,1)} async-done(((bf16[1,640,1024]{2,1,0:T(8,128)(2,1)}), bf16[1,160,1024]{2,1,0:T(8,128)(2,1)}) %reduce-scatter.9.cloned.1.call-update) | async-done | bytes 327696 | tf_op jit(solution)/shard_map/reduce_scatter | solution.py:41
  237.7 31.3 %all-gather.11.cloned.1.call-done = bf16[1,640,1024]{2,1,0:T(8,128)(2,1)} async-done(((bf16[1,160,1024]{2,1,0:T(8,128)(2,1)}), bf16[1,640,1024]{2,1,0:T(8,128)(2,1)}) %all-gather.11.cloned.1.call-update) | async-done | bytes 1310736 | tf_op jit(solution)/shard_map/all_gather | solution.py:496
  269.0 1.9 fusion.34
  270.9 5.0 %fusion.61 = (f32[4,64]{1,0:T(4,128)S(1)}, bf16[1,640,4,64]{1,3,2,0:T(8,128)(2,1)}) fusion(bf16[640,4,64]{0,2,1:T(8,128)(2,1)S(1)} %bitcast.158, f32[4,640,640]{1,2,0:T(8,128)} %copy-done, f32[4,640]{1,0:T(4,128)S(1)} %log_add_fusion), kind=kOutput, calls=%fused_computation.118 | convolution fusion | flops 213319424 | bytes 7220224 | tf_op jit(solution)/shard_map/shqk,sqhe->skhe/dot_general | solution.py:518
  275.9 4.5 %multiply_reduce_fusion = (f32[4,640]{1,0:T(4,128)S(1)}, f32[4,640,640]{1,2,0:T(8,128)S(1)}) fusion(f32[4,640,640]{1,2,0:T(8,128)} %copy-done, f32[4,640]{1,0:T(4,128)S(1)} %log_add_fusion, bf16[640,4,64]{0,2,1:T(8,128)(2,1)S(1)} %bitcast.159, bf16[640,4,64]{0,2,1:T(8,128)(2,1)S(1)} %bitcast.157), kind=kOutput, calls=%fused_computation.1 | convolution fusion | flops 214627840 | bytes 13783040 | tf_op jit(solution)/shard_map/sqhe,skhe->shqk/dot_general | solution.py:507
  284.6 2.3 fusion.12
  286.9 4.6 %convolution_convert_fusion = bf16[1024,1024]{1,0:T(8,128)(2,1)} fusion(bf16[640,1024]{1,0:T(8,128)(2,1)} %copy-done.23, bf16[1,640,1024]{2,1,0:T(8,128)(2,1)S(1)} %copy-done.22), kind=kOutput, calls=%fused_computation.19 | convolution fusion | flops 1343225856 | bytes 4718592 | tf_op jit(solution)/shard_map/bct,bcm->tm/dot_general | solution.py:461
  291.6 3.2 convolution_convert_fusion.1
  294.7 47.6 %shard_map.190 = (bf16[2,256,1024]{2,1,0:T(8,128)(2,1)}, bf16[2,512,512]{2,1,0:T(8,128)(2,1)}) custom-call(bf16[2,2,256,1024]{3,2,1,0:T(8,128)(2,1)} %bitcast.154, bf16[2,512,1024]{2,1,0:T(8,128)(2,1)} %bitcast.153), custom_call_target="tpu_custom_call" | custom-call | bytes 125829120 | tf_op jit(solution)/shard_map/pallas_call | solution.py:282
  342.3 2.9 bitcast_convert_fusion.1
  345.2 1.7 bitcast_convert_fusion
  348.3 12.8 %shard_map.189 = f32[64,128]{1,0:T(8,128)} custom-call(f32[48,128]{1,0:T(8,128)} %reshape.474.shared, f32[16,128]{1,0:T(8,128)} %fusion.52.local), custom_call_target="tpu_custom_call" | custom-call | bytes 20000000 | tf_op jit(solution)/shard_map/pallas_call | solution.py:350
  361.2 2.7 fusion.11
  363.9 1.6 copy.34
  365.6 2.7 fusion.26
  368.3 30.8 %shard_map.188 = (bf16[2,256,768]{2,1,0:T(8,128)(2,1)}, bf16[2,128,512]{2,1,0:T(8,128)(2,1)}) custom-call(bf16[2,2,256,768]{3,2,1,0:T(8,128)(2,1)} %bitcast.147, bf16[2,128,1024]{2,1,0:T(8,128)(2,1)} %bitcast.155), custom_call_target="tpu_custom_call" | custom-call | bytes 62914560 | tf_op jit(solution)/shard_map/pallas_call | solution.py:282
  399.1 2.5 reshape.486
  406.3 1.9 convert_add_fusion
  (142 shorter events, 32.4 us)
Async XLA Ops:
  7.2 6.0 %copy-start.16 = (bf16[512]{0:T(512)(128)(2,1)S(1)}, bf16[512]{0:T(512)(128)(2,1)}, u32[]{:S(2)}) copy-start(bf16[512]{0:T(512)(128)(2,1)} %param.18) | copy-start | bytes 3076
  7.2 6.0 %copy-start.17 = (bf16[2,128]{1,0:T(2,128)(2,1)S(1)}, bf16[2,128]{1,0:T(2,128)(2,1)}, u32[]{:S(2)}) copy-start(bf16[2,128]{1,0:T(2,128)(2,1)} %param.15) | copy-start | bytes 1540
  7.2 38.2 %all-gather.5.cloned.1.call-start = ((), (), s32[]{:S(2)}) async-start(), calls=%async_computation.4 | async-start | bytes 1638400 | tf_op jit(solution)/shard_map/all_gather | solution.py:382
  9.1 77.4 %reduce-scatter.5.cloned.1.call-start = ((), (), s32[]{:S(2)}) async-start(), calls=%async_computation.5 | async-start | bytes 1638400 | tf_op jit(solution)/shard_map/reduce_scatter | solution.py:41
  10.6 23.5 %copy-start.15 = (s32[1,640]{1,0:T(1,128)S(1)}, s32[1,640]{1,0:T(1,128)}, u32[]{:S(2)}) copy-start(s32[1,640]{1,0:T(1,128)} %param.12) | copy-start | bytes 7684
  48.8 2.3 copy-start.3
  50.2 2.7 copy-start
  54.2 33.4 %copy-start.5 = (bf16[4,64,640]{2,1,0:T(8,128)(2,1)}, bf16[4,64,640]{2,1,0:T(8,128)(2,1)S(1)}, u32[]{:S(2)}) copy-start(bf16[4,64,640]{2,1,0:T(8,128)(2,1)S(1)} %fusion.37) | copy-start | bytes 983044
  54.3 32.3 %copy-start.1 = (f32[1,160,1024]{2,1,0:T(8,128)S(1)}, f32[1,160,1024]{2,1,0:T(8,128)}, u32[]{:S(2)}) copy-start(f32[1,160,1024]{2,1,0:T(8,128)} %param.11) | copy-start | bytes 1966084
  55.9 64.3 %all-gather.7.cloned.1.call-start = ((), (), s32[]{:S(2)}) async-start(), calls=%async_computation.6 | async-start | bytes 1638400 | tf_op jit(solution)/shard_map/all_gather | solution.py:443
  88.8 71.1 %reduce-scatter.7.cloned.1.call-start = ((), (), s32[]{:S(2)}) async-start(), calls=%async_computation.7 | async-start | bytes 1638400 | tf_op jit(solution)/shard_map/reduce_scatter | solution.py:41
  120.2 6.5 %copy-start.19 = (bf16[1024,1024]{1,0:T(8,128)(2,1)S(1)}, bf16[1024,1024]{1,0:T(8,128)(2,1)}, u32[]{:S(2)}) copy-start(bf16[1024,1024]{1,0:T(8,128)(2,1)} %get-tuple-element.29) | copy-start | bytes 6291460
  129.3 32.2 %copy-start.2 = (f32[1,160,1024]{2,1,0:T(8,128)S(1)}, f32[1,160,1024]{2,1,0:T(8,128)}, u32[]{:S(2)}) copy-start(f32[1,160,1024]{2,1,0:T(8,128)} %param.13) | copy-start | bytes 1966084
  129.3 65.2 %all-gather.9.cloned.1.call-start = ((), (), s32[]{:S(2)}) async-start(), calls=%async_computation.8 | async-start | bytes 1638400 | tf_op jit(solution)/shard_map/all_gather | solution.py:458
  163.1 71.0 %reduce-scatter.9.cloned.1.call-start = ((), (), s32[]{:S(2)}) async-start(), calls=%async_computation.9 | async-start | bytes 1638400 | tf_op jit(solution)/shard_map/reduce_scatter | solution.py:41
  194.5 6.3 %copy-start.18 = (bf16[1024,1024]{1,0:T(8,128)(2,1)S(1)}, bf16[1024,1024]{1,0:T(8,128)(2,1)}, u32[]{:S(2)}) copy-start(bf16[1024,1024]{1,0:T(8,128)(2,1)} %get-tuple-element.28) | copy-start | bytes 6291460
  203.5 65.5 %all-gather.11.cloned.1.call-start = ((), (), s32[]{:S(2)}) async-start(), calls=%async_computation.10 | async-start | bytes 1638400 | tf_op jit(solution)/shard_map/all_gather | solution.py:496
  235.5 33.5 %copy-start.9 = (bf16[256,1024]{1,0:T(8,128)(2,1)S(1)}, bf16[256,1024]{1,0:T(8,128)(2,1)}, u32[]{:S(2)}) copy-start(bf16[256,1024]{1,0:T(8,128)(2,1)} %get-tuple-element.24) | copy-start | bytes 1572868
  237.6 168.7 %reduce-scatter.11.cloned.1.call-start = ((), (), s32[]{:S(2)}) async-start(), calls=%async_computation.11 | async-start | bytes 1638400 | tf_op jit(solution)/shard_map/reduce_scatter | solution.py:41
  270.9 5.0 %copy-start.4 = (bf16[1,640,256]{1,2,0:T(8,128)(2,1)S(1)}, bf16[1,640,256]{1,2,0:T(8,128)(2,1)}, u32[]{:S(2)}) copy-start(bf16[1,640,256]{1,2,0:T(8,128)(2,1)} %copy-done.3) | copy-start | bytes 983044
  270.9 9.5 %slice-start = ((s8[6553600]{0:T(1024)(128)(4,1)}), s8[4194304]{0:T(1024)(128)(4,1)S(1)}, s32[]{:S(2)}) async-start(s8[6553600]{0:T(1024)(128)(4,1)} %bitcast.145), calls=%async_computation.12 | async-start | bytes 8388608
  275.9 4.5 %slice-start.1 = ((s8[6553600]{0:T(1024)(128)(4,1)}), s8[2359296]{0:T(1024)(128)(4,1)S(1)}, s32[]{:S(2)}) async-start(s8[6553600]{0:T(1024)(128)(4,1)} %bitcast.145), calls=%async_computation.13 | async-start | bytes 4718592
  282.9 1.6 copy-start.20
  284.6 2.4 copy-start.22
  286.9 4.7 %copy-start.21 = (bf16[1,640,1024]{2,1,0:T(8,128)(2,1)S(1)}, bf16[1,640,1024]{2,1,0:T(8,128)(2,1)}, u32[]{:S(2)}) copy-start(bf16[1,640,1024]{2,1,0:T(8,128)(2,1)} %all-gather.7.cloned.1.call-done) | copy-start | bytes 3932164
  286.9 4.6 %copy-start.25 = (bf16[640,1024]{1,0:T(8,128)(2,1)S(1)}, bf16[640,1024]{1,0:T(8,128)(2,1)}, u32[]{:S(2)}) copy-start(bf16[640,1024]{1,0:T(8,128)(2,1)} %copy-done.24) | copy-start | bytes 3932164
  342.3 2.9 copy-start.7
  345.2 16.0 %copy-start.12 = (bf16[4,64,640]{2,1,0:T(8,128)(2,1)S(1)}, bf16[4,64,640]{2,1,0:T(8,128)(2,1)}, u32[]{:S(2)}) copy-start(bf16[4,64,640]{2,1,0:T(8,128)(2,1)} %copy-done.11) | copy-start | bytes 983044
  363.9 1.6 slice-start.4
  363.9 1.6 slice-start.3
  363.9 1.6 copy-start.6
  401.6 3.9 copy-start.13
  (7 other events, 8.4 us)
Sparse Core Ops, SparseCore 0:
  10.1 35.2 all-gather.4
  56.0 30.4 reduce-scatter.4
  89.0 31.1 all-gather.6
  129.4 30.4 reduce-scatter.6
  163.2 31.1 all-gather.8
  203.6 30.4 reduce-scatter.8
  237.7 31.1 all-gather.10
  287.0 30.4 reduce-scatter.10

commit v3 on v2

--- a/solution.py
+++ b/solution.py
@@ -458,9 +458,6 @@
     second_gradient_full = lax.all_gather(
         d_second.astype(jnp.bfloat16), "tensor", axis=1, tiled=True
     )
-    down_weight_gradient = jnp.einsum(
-        "bct,bcm->tm", activation_bfloat, second_gradient_full, preferred_element_type=jnp.float32
-    )
     d_pre = (
         jnp.einsum(
             "ajn,tn->ajt",
@@ -478,9 +475,18 @@
     hidden_state_slice = jnp.einsum(
         "ixj,gj->ixg", preact_gradient_bfloat, up_weight_full, preferred_element_type=jnp.float32
     )
-    d_hidden = (
-        scatter_sum(hidden_state_slice, "tensor", 1).astype(jnp.float32) + d_second
-    )
+    bf = jnp.bfloat16
+    hidden_state_slice, activation_late = lax.optimization_barrier(
+        (hidden_state_slice.astype(bf), activation_bfloat)
+    )
+    down_weight_gradient = jnp.einsum(
+        "bct,bcm->tm", activation_late, second_gradient_full, preferred_element_type=jnp.float32
+    )
+    (grad_down,) = sum_grads((down_weight_gradient.astype(bf),), (1,), 3)
+    hidden_scattered, grad_down = lax.optimization_barrier(
+        (scatter_sum(hidden_state_slice, "tensor", 1), grad_down)
+    )
+    d_hidden = hidden_scattered.astype(jnp.float32) + d_second
     d_first = norm_backward(d_hidden, normed_one, inverse_one, gain_full[0])
     gain_part = jnp.stack(
         [jnp.sum(d_hidden * normed_one, axis=(0, 1)), jnp.sum(grad_out * normed_two, axis=(0, 1))]
@@ -493,7 +499,13 @@
             jnp.sum(grad_out, axis=(0, 1)),
         ]
     )
-    first_gradient_full = lax.all_gather(d_first.astype(jnp.bfloat16), "tensor", axis=1, tiled=True)
+    d_first_bf, up_weight_gradient = lax.optimization_barrier(
+        (d_first.astype(bf), up_weight_gradient.astype(bf))
+    )
+    (grad_up,) = sum_grads((up_weight_gradient,), (0,), 4)
+    first_gradient_full, grad_up = lax.optimization_barrier(
+        (lax.all_gather(d_first_bf, "tensor", axis=1, tiled=True), grad_up)
+    )
     output_weight_gradient = jnp.einsum(
         "unb,una->ba", attention_context, first_gradient_full, preferred_element_type=jnp.float32
     )
@@ -526,12 +538,12 @@
     d_values = d_values.reshape(seqs, length, cols)
     g_qv = jnp.stack([jnp.sum(d_query, axis=(0, 1)), jnp.sum(d_values, axis=(0, 1))])
     projected_gradient_bfloat = jnp.concatenate([d_query, d_keys, d_values], axis=2).astype(jnp.bfloat16)
-    projection_weight_gradient = jnp.einsum(
-        "pjx,pjv->xv",
-        input_rows_full,
-        projected_gradient_bfloat,
-        preferred_element_type=jnp.float32,
-    )
+    projection_parts = [
+        jnp.einsum(
+            "pjx,pjv->xv", input_rows_full, part.astype(bf), preferred_element_type=jnp.float32
+        )
+        for part in (d_query, d_keys, d_values)
+    ]
     input_slice = jnp.einsum(
         "pxv,yv->pxy",
         projected_gradient_bfloat,
@@ -539,17 +551,16 @@
         preferred_element_type=jnp.float32,
     )
     grad_in = scatter_sum(input_slice, "tensor", 1).astype(jnp.float32) + d_first
-    bf = jnp.bfloat16
-    grad_up, grad_down = sum_grads(
-        (up_weight_gradient.astype(bf), down_weight_gradient.astype(bf)), (0, 1), 3
-    )
-    grad_qkv_flat, grad_out_weight = sum_grads(
-        (projection_weight_gradient.astype(bf), output_weight_gradient.astype(bf)), (0, 1), 4
-    )
-    grad_qkv = grad_qkv_flat.reshape(-1, 3, cols)
+    grad_q, grad_k, grad_v, grad_out_weight = sum_grads(
+        tuple(part.astype(bf) for part in projection_parts)
+        + (output_weight_gradient.astype(bf),),
+        (0, 0, 0, 1),
+        5,
+    )
+    grad_qkv = jnp.stack([grad_q, grad_k, grad_v], axis=1)
     shard_index = lax.axis_index("shard")
     shared = as_rows(jnp.concatenate([gain_part, shift_part]))
-    sums = sum_small(shared, as_rows(jnp.concatenate([g_qv.reshape(-1), g_upbias])), 5)
+    sums = sum_small(shared, as_rows(jnp.concatenate([g_qv.reshape(-1), g_upbias])), 6)
     wide = sums[: shared.shape[0]].reshape(-1)[: 6 * width].reshape(6, width)
     gain_tot, shift_tot = wide[:2], wide[2:]
     own = sums[shared.shape[0] :].reshape(-1)

time: 416 us -> 373 us (0.90)
  waiting for transfers between devices: 166 us -> 104 us
  Pallas kernels: 141 us -> 158 us
    all_gather x1, waiting for transfers between devices: 31.3 us -> 0.01 us  [shards(): lax.all_gather(d_first_bf, 'tensor', axis=1, tiled=True)]
    reduce_scatter x4, waiting for transfers between devices: 91.6 us -> 61 us  [scatter_sum(): lax.psum_scatter(part.astype(jnp.bfloat16), axes, scatter_dimension=dim,...]
    pallas_call x2 -> x3, Pallas kernels: 78.3 us -> 94.6 us  [sum_grads(): pl.pallas_call(functools.partial(grad_kernel, n, m, kinds), out_shape=out...]
    unnamed x64 -> x61, local copies, waits for them, and re-layouts: 10 us -> 8.56 us
  transfers between devices with their start and end apart: 8 -> 8, of which waited for: 7 -> 5; matrix products, arithmetic and copies ran while one was open for 8% -> 9% of each run, Pallas kernels for 34% -> 43%
where the time goes in v3:
time: 373 us; the launch traced here: 372 us
  Pallas kernels  158 us (42%)
  waiting for transfers between devices  104 us (28%)
  matrix products  52.4 us (14%)
  other arithmetic  25.6 us (7%)
  local copies, waits for them, and re-layouts  16.1 us (4%)
  between operations  14.7 us (4%)
    pallas_call x3, Pallas kernels, sum_grads(): pl.pallas_call(functools.partial(grad_kernel, n, m, kinds), out_shape=out...  94.6 us
    reduce_scatter x4, waiting for transfers between devices, scatter_sum(): lax.psum_scatter(part.astype(jnp.bfloat16), axes, scatter_dimension=dim,...  61 us
    pallas_call x2, Pallas kernels, gather_blocks(): pl.pallas_call(functools.partial(gather_kernel, n, kinds, shapes), out_sh...  50 us
    all_gather x1, waiting for transfers between devices, shards(): lax.all_gather(d_second.astype(jnp.bfloat16), 'tensor', axis=1, tiled=True)  31.1 us
    pallas_call x1, Pallas kernels, sum_small(): pl.pallas_call(functools.partial(small_kernel, sizes), out_shape=jax.Shap...  13.5 us
    all_gather x1, waiting for transfers between devices, shards(): input_rows_full = lax.all_gather(inputs_bf, 'tensor', axis=1, tiled=True)  11.1 us
    unnamed x61, local copies, waits for them, and re-layouts  8.56 us
  transfers between devices with their start and end apart: 8, of which 5 were waited for; matrix products, arithmetic and copies ran while one was open for 9% of the time, Pallas kernels for 43%

profile of v3, /device:TPU:0, one launch (start us, length us, event | category | flops | bytes accessed | tf_op | source)
XLA Modules:
  0.0 371.7 jit_solution(7342293314850515212)
XLA Ops:
  7.2 1.9 convert_element_type.189
  10.6 1.4 copy.29
  13.8 19.4 %shard_map.186 = (bf16[1024,768]{1,0:T(8,128)(2,1)}, bf16[256,1024]{1,0:T(8,128)(2,1)}, f32[2,32,128]{2,1,0:T(8,128)}) custom-call(bf16[512,768]{1,0:T(8,128)(2,1)} %copy.30.refs_0_, bf16[256,512]{1,0:T(8,128)(2,1)} %refs_1_.1, f32[32,128]{1,0:T(8,128)} %fusion.79.refs_2_), custom_call_target="tpu_custom_call" | custom-call | bytes 42598400 | tf_op jit(solution)/shard_map/pallas_call | solution.py:137
  34.4 11.1 %all-gather.5.cloned.1.call-done = bf16[1,640,1024]{2,1,0:T(8,128)(2,1)} async-done(((bf16[1,160,1024]{2,1,0:T(8,128)(2,1)}), bf16[1,640,1024]{2,1,0:T(8,128)(2,1)}) %all-gather.5.cloned.1.call-update) | async-done | bytes 1310736 | tf_op jit(solution)/shard_map/all_gather | solution.py:382
  45.4 3.2 convolution_bitcast_fusion.1
  51.1 1.8 copy-done
  54.3 1.6 convolution_bitcast_fusion
  56.1 30.5 %reduce-scatter.5.cloned.1.call-done = bf16[1,160,1024]{2,1,0:T(8,128)(2,1)} async-done(((bf16[1,640,1024]{2,1,0:T(8,128)(2,1)}), bf16[1,160,1024]{2,1,0:T(8,128)(2,1)}) %reduce-scatter.5.cloned.1.call-update) | async-done | bytes 327696 | tf_op jit(solution)/shard_map/reduce_scatter | solution.py:41
  88.9 30.5 %shard_map.187 = (bf16[1024,1024]{1,0:T(8,128)(2,1)}, bf16[1024,1024]{1,0:T(8,128)(2,1)}) custom-call(bf16[512,1024]{1,0:T(8,128)(2,1)} %refs_0_, bf16[1024,512]{1,0:T(8,128)(2,1)} %refs_1_.2), custom_call_target="tpu_custom_call" | custom-call | bytes 83886080 | tf_op jit(solution)/shard_map/pallas_call | solution.py:137
  120.2 5.4 %multiply_convert_fusion.1 = (bf16[640,1024]{1,0:T(8,128)(2,1)S(1)}, f32[640,1024]{1,0:T(8,128)}) fusion(f32[1024]{0:T(1024)S(1)} %bitcast.235, bf16[1024,1024]{1,0:T(8,128)(2,1)} %get-tuple-element.36, bf16[1,640,1024]{2,1,0:T(8,128)(2,1)} %all-gather.7.cloned.1.call-done), kind=kOutput, calls=%fused_computation.17 | convolution fusion | flops 1346109440 | bytes 7344128 | tf_op jit(solution)/shard_map/peo,ot->pet/dot_general | solution.py:444
  126.7 2.6 fusion.12
  129.3 30.6 %reduce-scatter.7.cloned.1.call-done = bf16[1,160,1024]{2,1,0:T(8,128)(2,1)} async-done(((bf16[1,640,1024]{2,1,0:T(8,128)(2,1)}), bf16[1,160,1024]{2,1,0:T(8,128)(2,1)}) %reduce-scatter.7.cloned.1.call-update) | async-done | bytes 327696 | tf_op jit(solution)/shard_map/reduce_scatter | solution.py:41
  163.3 31.1 %all-gather.9.cloned.1.call-done = bf16[1,640,1024]{2,1,0:T(8,128)(2,1)} async-done(((bf16[1,160,1024]{2,1,0:T(8,128)(2,1)}), bf16[1,640,1024]{2,1,0:T(8,128)(2,1)}) %all-gather.9.cloned.1.call-update) | async-done | bytes 1310736 | tf_op jit(solution)/shard_map/all_gather | solution.py:458
  194.5 5.3 %fusion.93 = (f32[1024]{0:T(1024)S(1)}, bf16[640,1024]{1,0:T(8,128)(2,1)S(1)}) fusion(f32[640,1024]{1,0:T(8,128)} %get-tuple-element.85, f32[1024]{0:T(1024)S(1)} %bitcast.236, bf16[1024,1024]{1,0:T(8,128)(2,1)} %get-tuple-element.37, bf16[1,640,1024]{2,1,0:T(8,128)(2,1)} %all-gather.9.cloned.1.call-done), kind=kOutput, calls=%fused_computation.137 | convolution fusion | flops 1350040576 | bytes 7348224 | tf_op jit(solution)/shard_map/ajn,tn->ajt/dot_general | solution.py:462
  200.8 2.6 fusion.13
  203.5 4.9 %convolution_convert_fusion.1 = bf16[1024,1024]{1,0:T(8,128)(2,1)} fusion(bf16[1,640,1024]{2,1,0:T(8,128)(2,1)} %bitcast.239, bf16[1,640,1024]{2,1,0:T(8,128)(2,1)} %all-gather.9.cloned.1.call-done), kind=kOutput, calls=%fused_computation.20 | convolution fusion | flops 1343225856 | bytes 4718592 | tf_op jit(solution)/shard_map/bct,bcm->tm/dot_general | solution.py:482
  208.4 35.5 %shard_map.188 = bf16[2,512,512]{2,1,0:T(8,128)(2,1)} custom-call(bf16[2,512,1024]{2,1,0:T(8,128)(2,1)} %bitcast.184), custom_call_target="tpu_custom_call" | custom-call | bytes 62914560 | tf_op jit(solution)/shard_map/pallas_call | solution.py:282
  243.9 3.0 bitcast_convert_fusion.1
  246.9 3.2 convolution_convert_fusion
  250.0 1.4 multiply_reduce_fusion.2
  253.8 33.9 %shard_map.189 = bf16[2,256,1024]{2,1,0:T(8,128)(2,1)} custom-call(bf16[2,2,256,1024]{3,2,1,0:T(8,128)(2,1)} %bitcast.183), custom_call_target="tpu_custom_call" | custom-call | bytes 62914560 | tf_op jit(solution)/shard_map/pallas_call | solution.py:282
  287.8 2.8 bitcast_convert_fusion
  290.6 1.9 fusion.57
  292.6 5.0 %fusion.88 = (f32[4,64]{1,0:T(4,128)S(1)}, bf16[1,640,4,64]{1,3,2,0:T(8,128)(2,1)}) fusion(bf16[640,4,64]{0,2,1:T(8,128)(2,1)S(1)} %bitcast.193, f32[4,640,640]{1,2,0:T(8,128)} %copy-done, f32[4,640]{1,0:T(4,128)S(1)} %log_add_fusion), kind=kOutput, calls=%fused_computation.132 | convolution fusion | flops 213319424 | bytes 7220224 | tf_op jit(solution)/shard_map/shqk,sqhe->skhe/dot_general | solution.py:530
  297.5 4.5 %multiply_reduce_fusion = (f32[4,640]{1,0:T(4,128)S(1)}, f32[4,640,640]{1,2,0:T(8,128)S(1)}) fusion(f32[4,640,640]{1,2,0:T(8,128)} %copy-done, f32[4,640]{1,0:T(4,128)S(1)} %log_add_fusion, bf16[640,4,64]{0,2,1:T(8,128)(2,1)S(1)} %bitcast.194, bf16[640,4,64]{0,2,1:T(8,128)(2,1)S(1)} %bitcast.190), kind=kOutput, calls=%fused_computation.1 | convolution fusion | flops 214627840 | bytes 13783040 | tf_op jit(solution)/shard_map/sqhe,skhe->shqk/dot_general | solution.py:519
  306.2 2.3 fusion.11
  310.0 13.5 %shard_map.191 = f32[64,128]{1,0:T(8,128)} custom-call(f32[48,128]{1,0:T(8,128)} %reshape.532.shared, f32[16,128]{1,0:T(8,128)} %fusion.80.local), custom_call_target="tpu_custom_call" | custom-call | bytes 20000000 | tf_op jit(solution)/shard_map/pallas_call | solution.py:350
  325.2 1.6 fusion.50
  330.0 2.7 fusion.40
  332.8 25.2 %shard_map.190 = (bf16[2,256,256]{2,1,0:T(8,128)(2,1)}, bf16[2,256,256]{2,1,0:T(8,128)(2,1)}, bf16[2,256,256]{2,1,0:T(8,128)(2,1)}, bf16[2,128,512]{2,1,0:T(8,128)(2,1)}) custom-call(bf16[2,2,256,256]{3,2,1,0:T(8,128)(2,1)} %bitcast.187, bf16[2,2,256,256]{3,2,1,0:T(8,128)(2,1)} %bitcast.186, bf16[2,2,256,256]{3,2,1,0:T(8,128)(2,1)} %bitcast.185, ...), custom_call_target="tpu_custom_call" | custom-call | bytes 62914560 | tf_op jit(solution)/shard_map/pallas_call | solution.py:282
  359.8 2.4 maximum_convert_fusion
  363.0 1.9 convert_add_fusion
  (144 shorter events, 32.5 us)
Async XLA Ops:
  7.2 6.0 %copy-start.16 = (bf16[512]{0:T(512)(128)(2,1)S(1)}, bf16[512]{0:T(512)(128)(2,1)}, u32[]{:S(2)}) copy-start(bf16[512]{0:T(512)(128)(2,1)} %param.18) | copy-start | bytes 3076
  7.2 6.0 %copy-start.17 = (bf16[2,128]{1,0:T(2,128)(2,1)S(1)}, bf16[2,128]{1,0:T(2,128)(2,1)}, u32[]{:S(2)}) copy-start(bf16[2,128]{1,0:T(2,128)(2,1)} %param.15) | copy-start | bytes 1540
  7.2 38.2 %all-gather.5.cloned.1.call-start = ((), (), s32[]{:S(2)}) async-start(), calls=%async_computation.4 | async-start | bytes 1638400 | tf_op jit(solution)/shard_map/all_gather | solution.py:382
  9.1 77.4 %reduce-scatter.5.cloned.1.call-start = ((), (), s32[]{:S(2)}) async-start(), calls=%async_computation.5 | async-start | bytes 1638400 | tf_op jit(solution)/shard_map/reduce_scatter | solution.py:41
  10.6 23.5 %copy-start.15 = (s32[1,640]{1,0:T(1,128)S(1)}, s32[1,640]{1,0:T(1,128)}, u32[]{:S(2)}) copy-start(s32[1,640]{1,0:T(1,128)} %param.12) | copy-start | bytes 7684
  48.8 2.3 copy-start.4
  50.2 2.7 copy-start
  54.3 33.4 %copy-start.6 = (bf16[4,64,640]{2,1,0:T(8,128)(2,1)}, bf16[4,64,640]{2,1,0:T(8,128)(2,1)S(1)}, u32[]{:S(2)}) copy-start(bf16[4,64,640]{2,1,0:T(8,128)(2,1)S(1)} %fusion.60) | copy-start | bytes 983044
  54.3 32.3 %copy-start.2 = (f32[1,160,1024]{2,1,0:T(8,128)S(1)}, f32[1,160,1024]{2,1,0:T(8,128)}, u32[]{:S(2)}) copy-start(f32[1,160,1024]{2,1,0:T(8,128)} %param.11) | copy-start | bytes 1966084
  55.9 64.3 %all-gather.7.cloned.1.call-start = ((), (), s32[]{:S(2)}) async-start(), calls=%async_computation.6 | async-start | bytes 1638400 | tf_op jit(solution)/shard_map/all_gather | solution.py:443
  88.8 71.1 %reduce-scatter.7.cloned.1.call-start = ((), (), s32[]{:S(2)}) async-start(), calls=%async_computation.7 | async-start | bytes 1638400 | tf_op jit(solution)/shard_map/reduce_scatter | solution.py:41
  120.2 6.4 %copy-start.19 = (bf16[1024,1024]{1,0:T(8,128)(2,1)S(1)}, bf16[1024,1024]{1,0:T(8,128)(2,1)}, u32[]{:S(2)}) copy-start(bf16[1024,1024]{1,0:T(8,128)(2,1)} %get-tuple-element.37) | copy-start | bytes 6291460
  129.3 32.2 %copy-start.3 = (f32[1,160,1024]{2,1,0:T(8,128)S(1)}, f32[1,160,1024]{2,1,0:T(8,128)}, u32[]{:S(2)}) copy-start(f32[1,160,1024]{2,1,0:T(8,128)} %param.13) | copy-start | bytes 1966084
  129.3 65.2 %all-gather.9.cloned.1.call-start = ((), (), s32[]{:S(2)}) async-start(), calls=%async_computation.8 | async-start | bytes 1638400 | tf_op jit(solution)/shard_map/all_gather | solution.py:458
  163.1 86.9 %reduce-scatter.9.cloned.1.call-start = ((), (), s32[]{:S(2)}) async-start(), calls=%async_computation.9 | async-start | bytes 1638400 | tf_op jit(solution)/shard_map/reduce_scatter | solution.py:41
  194.5 6.3 %copy-start.18 = (bf16[1024,1024]{1,0:T(8,128)(2,1)S(1)}, bf16[1024,1024]{1,0:T(8,128)(2,1)}, u32[]{:S(2)}) copy-start(bf16[1024,1024]{1,0:T(8,128)(2,1)} %get-tuple-element.36) | copy-start | bytes 6291460
  203.4 87.2 %all-gather.11.cloned.1.call-start = ((), (), s32[]{:S(2)}) async-start(), calls=%async_computation.10 | async-start | bytes 1638400 | tf_op jit(solution)/shard_map/all_gather | solution.py:507
  243.8 3.0 copy-start.21
  243.9 3.0 copy-start.24
  253.5 109.5 %reduce-scatter.11.cloned.1.call-start = ((), (), s32[]{:S(2)}) async-start(), calls=%async_computation.11 | async-start | bytes 1638400 | tf_op jit(solution)/shard_map/reduce_scatter | solution.py:41
  287.8 2.9 copy-start.12
  292.5 5.0 %copy-start.5 = (bf16[1,640,256]{1,2,0:T(8,128)(2,1)S(1)}, bf16[1,640,256]{1,2,0:T(8,128)(2,1)}, u32[]{:S(2)}) copy-start(bf16[1,640,256]{1,2,0:T(8,128)(2,1)} %copy-done.4) | copy-start | bytes 983044
  292.6 9.5 %slice-start = ((s8[6553600]{0:T(1024)(128)(4,1)}), s8[4194304]{0:T(1024)(128)(4,1)S(1)}, s32[]{:S(2)}) async-start(s8[6553600]{0:T(1024)(128)(4,1)} %bitcast.176), calls=%async_computation.12 | async-start | bytes 8388608
  297.5 4.5 %slice-start.1 = ((s8[6553600]{0:T(1024)(128)(4,1)}), s8[2359296]{0:T(1024)(128)(4,1)S(1)}, s32[]{:S(2)}) async-start(s8[6553600]{0:T(1024)(128)(4,1)} %bitcast.176), calls=%async_computation.13 | async-start | bytes 4718592
  304.6 4.0 %copy-start.10 = (bf16[4,64,640]{2,1,0:T(8,128)(2,1)}, bf16[4,64,640]{2,1,0:T(8,128)(2,1)S(1)}, u32[]{:S(2)}) copy-start(bf16[4,64,640]{2,1,0:T(8,128)(2,1)S(1)} %fusion.56) | copy-start | bytes 983044
  306.2 17.3 %copy-start.1 = (bf16[1,640,1024]{2,1,0:T(8,128)(2,1)S(1)}, bf16[1,640,1024]{2,1,0:T(8,128)(2,1)}, u32[]{:S(2)}) copy-start(bf16[1,640,1024]{2,1,0:T(8,128)(2,1)} %all-gather.5.cloned.1.call-done) | copy-start | bytes 3932164
  306.2 17.3 %copy-start.9 = (bf16[1,640,4,64]{1,3,2,0:T(8,128)(2,1)S(1)}, bf16[1,640,4,64]{1,3,2,0:T(8,128)(2,1)}, u32[]{:S(2)}) copy-start(bf16[1,640,4,64]{1,3,2,0:T(8,128)(2,1)} %get-tuple-element.73) | copy-start | bytes 983044
  323.5 1.7 slice-start.4
  323.5 1.7 slice-start.3
  326.8 2.6 copy-start.14
  326.8 3.3 copy-start.7
  358.0 4.2 %copy-start.13 = (bf16[2,128,512]{2,1,0:T(8,128)(2,1)S(1)}, bf16[2,128,512]{2,1,0:T(8,128)(2,1)}, u32[]{:S(2)}) copy-start(bf16[2,128,512]{2,1,0:T(8,128)(2,1)} %get-tuple-element.47) | copy-start | bytes 786436
  (6 other events, 7.8 us)
Sparse Core Ops, SparseCore 0:
  10.1 35.2 all-gather.4
  56.0 30.4 reduce-scatter.4
  89.0 31.1 all-gather.6
  129.4 30.4 reduce-scatter.6
  163.2 31.1 all-gather.8
  203.6 30.4 reduce-scatter.8
  253.6 30.5 all-gather.10
  308.7 30.6 reduce-scatter.10
